TPU v7x, 128 devices: a whole 4x4x4 slice. The times are simulated.
128 devices in a mesh: wide: 32 (over x, y_lo, z), narrow: 4 (over y_hi, core).
Axes of the slice: x: 4, y: 4 (y_hi: 2, y_lo: 2; y = y_hi * 2 + y_lo), z: 4, core: 2. Of those that a mesh axis runs over, the one named last changes fastest.
Arguments:
- force_columns: float32 [32, 64, 32, 16, 256], P('wide', 'narrow'), may hold values from -18 to 18
- coefficient: float32 [32, 64, 16, 256], P('wide', 'narrow'), may hold values from 0.1 to 10
- sweep_counts: int32 [32, 64], P('wide', 'narrow'), may hold values from 1 to 8, as said below
Outputs:
- self_block: float32 [32, 64, 1024], P('wide', 'narrow')
- row_block: float32 [32, 64, 1024], P('wide', 'narrow')
- column_block: float32 [32, 64, 1024], P('wide', 'narrow')
Inputs may be any that keep to these rules, and one draw needn't show every extreme that they name: `sweep_counts`: A brick takes either 8 sweeps or at most 2; bricks with 8 lie only in a quarter of the brick rows (at least one row), and some brick takes 8.
All inputs are finite; a program needn't handle non-finite values.
Results may differ from a plain program's by a relative error of at most 0.0003.
Values sent between devices are 32-bit elements; how exact they have to be, the bound alone decides.
A program may use at most 256 MiB of HBM per device.

v0:
```python
import jax
import jax.numpy as jnp
from jax import lax
from jax.sharding import PartitionSpec as P

MARGIN = 4


REACTION = 1.0
BOUND_LOW = 0.1
BOUND_HIGH = 2.0
CENTRE = 0.5 * (BOUND_LOW + BOUND_HIGH)
HALF_WIDTH = 0.5 * (BOUND_HIGH - BOUND_LOW)
SIGMA_RATIO = CENTRE / HALF_WIDTH


def from_behind(block, axis, distance):
    devices = range(lax.axis_size(axis))
    route = [((i - distance) % len(devices), i) for i in devices]
    return lax.ppermute(block, axis, route)


def prepare(coefficient):
    edge_len = coefficient.shape[-2]
    plane_len = coefficient.shape[-1]
    x_index = lax.broadcasted_iota(jnp.int32, (edge_len, plane_len), 0)
    flat_index = lax.broadcasted_iota(jnp.int32, (edge_len, plane_len), 1)
    y_index = flat_index // edge_len
    z_index = flat_index % edge_len
    x_next = jnp.concatenate([coefficient[..., 1:, :], coefficient[..., -1:, :]], axis=-2)
    x_prev = jnp.concatenate([coefficient[..., :1, :], coefficient[..., :-1, :]], axis=-2)
    y_next = jnp.concatenate([coefficient[..., edge_len:], coefficient[..., -edge_len:]], axis=-1)
    y_prev = jnp.concatenate([coefficient[..., :edge_len], coefficient[..., :-edge_len]], axis=-1)
    z_next = jnp.where(
        z_index == edge_len - 1,
        coefficient,
        jnp.concatenate([coefficient[..., 1:], coefficient[..., -1:]], axis=-1),
    )
    z_prev = jnp.where(
        z_index == 0,
        coefficient,
        jnp.concatenate([coefficient[..., :1], coefficient[..., :-1]], axis=-1),
    )
    faces = (
        (coefficient + x_next) * 0.5,
        (coefficient + x_prev) * 0.5,
        (coefficient + y_next) * 0.5,
        (coefficient + y_prev) * 0.5,
        (coefficient + z_next) * 0.5,
        (coefficient + z_prev) * 0.5,
    )
    diagonal = REACTION + faces[0]
    for face in faces[1:]:
        diagonal = diagonal + face
    keeps = (
        x_index < edge_len - 1,
        x_index > 0,
        y_index < edge_len - 1,
        y_index > 0,
        z_index < edge_len - 1,
        z_index > 0,
    )
    off_terms = tuple(
        (jnp.where(keep, face, jnp.zeros_like(face)) for keep, face in zip(keeps, faces))
    )
    return (diagonal, off_terms)


def neighbours(field):
    edge_len = field.shape[-2]
    zero_row = jnp.zeros_like(field[..., :1, :])
    zero_line = jnp.zeros_like(field[..., :edge_len])
    zero_cell = jnp.zeros_like(field[..., :1])
    return (
        jnp.concatenate([field[..., 1:, :], zero_row], axis=-2),
        jnp.concatenate([zero_row, field[..., :-1, :]], axis=-2),
        jnp.concatenate([field[..., edge_len:], zero_line], axis=-1),
        jnp.concatenate([zero_line, field[..., :-edge_len]], axis=-1),
        jnp.concatenate([field[..., 1:], zero_cell], axis=-1),
        jnp.concatenate([zero_cell, field[..., :-1]], axis=-1),
    )


def operate(field, diagonal, off_terms):
    result = diagonal * field
    for weight, shifted in zip(off_terms, neighbours(field)):
        result = result - weight * shifted
    return result


def start(force_block, coefficient):
    diagonal, off_terms = prepare(coefficient)
    diagonal = diagonal[:, None]
    off_terms = tuple((term[:, None] for term in off_terms))
    inverse = 1.0 / diagonal
    direction = force_block * inverse * (1.0 / CENTRE)
    rho_start = jnp.zeros((), jnp.float32) + 1.0 / SIGMA_RATIO
    return (
        (jnp.zeros_like(force_block), force_block, direction, rho_start),
        diagonal,
        off_terms,
        inverse,
    )


def sweep_step(sweep_index, carry_state, diagonal, off_terms, inverse, counts):
    snapshot, residual, direction, rho_value = carry_state
    live = (sweep_index < counts)[:, None, None, None]
    moved = snapshot + direction
    reduced = residual - operate(direction, diagonal, off_terms)
    rho_next = 1.0 / (2.0 * SIGMA_RATIO - rho_value)
    turned = rho_next * rho_value * direction + 2.0 * rho_next / HALF_WIDTH * (reduced * inverse)
    return (
        jnp.where(live, moved, snapshot),
        jnp.where(live, reduced, residual),
        jnp.where(live, turned, direction),
        rho_next,
    )


def run_bricks(force_block, coefficient, counts):
    carry_state, diagonal, off_terms, inverse = start(force_block, coefficient)
    highest = jnp.max(counts)

    def keep_going(loop_state):
        return loop_state[0] < highest

    def advance(loop_state):
        sweep_index = loop_state[0]
        return (
            sweep_index + 1,
            sweep_step(sweep_index, loop_state[1], diagonal, off_terms, inverse, counts),
        )

    finished = lax.while_loop(keep_going, advance, (jnp.zeros((), jnp.int32), carry_state))
    return finished[1][0]


def ramp(position, edge_len):
    return jnp.minimum(
        1.0, jnp.minimum((position + 0.5) / MARGIN, (edge_len - position - 0.5) / MARGIN)
    )


def partition(edge_len):
    x_index = lax.broadcasted_iota(jnp.int32, (edge_len, edge_len * edge_len), 0)
    flat_index = lax.broadcasted_iota(jnp.int32, (edge_len, edge_len * edge_len), 1)
    x_float = x_index.astype(jnp.float32)
    y_float = (flat_index // edge_len).astype(jnp.float32)
    return ramp(x_float, edge_len) * ramp(y_float, edge_len)


def on_device(force_columns, coefficient, sweep_counts):
    bricks = force_columns.shape[1]
    columns = force_columns.shape[2]
    edge_len = force_columns.shape[3]
    snapshot = run_bricks(force_columns[0], coefficient[0], sweep_counts[0])
    weighted = snapshot * partition(edge_len)
    scale_pair = (MARGIN * edge_len * edge_len) ** (-0.5)
    flattened = weighted.reshape(bricks, columns, -1)
    self_part = jnp.einsum(
        "bkc,blc->bkl", flattened, flattened, precision=lax.Precision.HIGHEST
    ) / float(edge_len**3)
    upper_slab = weighted[:, :, :MARGIN, :]
    below = from_behind(upper_slab, "wide", -1)
    lower_slab = weighted[:, :, edge_len - MARGIN :, :]
    row_part = (
        jnp.einsum("bkaj,blaj->bkl", lower_slab, below, precision=lax.Precision.HIGHEST)
        * scale_pair
    )
    cubed = weighted.reshape(bricks, columns, edge_len, edge_len, edge_len)
    front_slab = cubed[:, :, :, :MARGIN, :].reshape(bricks, columns, -1)
    back_slab = cubed[:, :, :, edge_len - MARGIN :, :].reshape(bricks, columns, -1)
    arrived = from_behind(front_slab[0], "narrow", -1)
    beside = jnp.concatenate([front_slab[1:], arrived[None]], axis=0)
    column_part = (
        jnp.einsum("bkc,blc->bkl", back_slab, beside, precision=lax.Precision.HIGHEST) * scale_pair
    )
    return (
        self_part.reshape(1, bricks, -1),
        row_part.reshape(1, bricks, -1),
        column_part.reshape(1, bricks, -1),
    )


def solution(mesh):
    in_specs = (
        P("wide", "narrow", None, None, None),
        P("wide", "narrow", None, None),
        P("wide", "narrow"),
    )
    out_specs = (P("wide", "narrow", None), P("wide", "narrow", None), P("wide", "narrow", None))
    return jax.shard_map(
        on_device, mesh=mesh, in_specs=in_specs, out_specs=out_specs, check_vma=False
    )
```

profile of v0, /device:TPU:27, one launch (start us, length us, event | category | flops | bytes accessed | tf_op | source)
XLA Modules:
  0.0 807.4 jit_solution(14070440561426641331)
XLA Ops:
  0.6 8.0 copy.148
  21.1 7.9 multiply_multiply_fusion
  34.0 673.8 %while.18 = (s32[]{:T(128)}, f32[16,32,16,256]{3,2,1,0:T(8,128)}, f32[16,32,16,256]{3,2,1,0:T(8,128)}, f32[16,32,16,256]{3,2,1,0:T(8,128)}, f32[]{:T(128)}, /*in...) while((s32[]{:T(128)}, f32[16,32,16,256]{3,2,1,0:T(8,128)}, ...), condition=%wide.region_2.3_spmd, body=%wide.region_1.2_spmd.sunk | while | flops 46137364 | bytes 272433568 | solution.py:135
  35.1 13.1 %fusion.50 = (f32[16,32,16,255]{3,2,1,0:T(8,128)}, f32[16,32,16,255]{3,2,1,0:T(8,128)}) fusion(f32[16,32,16,256]{3,2,1,0:T(8,128)} %get-tuple-element.453), kind=kLoop, calls=%fused_computation.93.clone.1 | loop fusion | bytes 33423360 | tf_op jit(solution)/shard_map/while/body/slice | solution.py:79
  48.3 7.3 fusion.51
  62.4 28.9 %add_select_fusion.3 = (f32[16,32,16,256]{3,2,1,0:T(8,128)}, f32[16,32,16,256]{3,2,1,0:T(8,128)}) fusion(f32[16,32,16,256]{3,2,1,0:T(8,128)} %get-tuple-element.453, f32[16,16,256]{2,1,0:T(8,128)S(1)} %bitcast.121, f32[]{:T(128)S(6)} %div.102, f32[]{:T(128)S(6)} %mul.491, pred[16]{0:T(512)(128)(4,1)S(1)} %broadcast_compare_fusion.2, ...), kind=kLoop, calls=%fused_computation.1.clone.1 | loop fusion | flops 39845888 | bytes 83820568 | tf_op jit(solution)/shard_map/while/body/jit(_where)/select_n | solution.py:116
  91.3 19.2 %broadcast_select_fusion.8 = (f32[16,32,16,256]{3,2,1,0:T(8,128)}, f32[16,32,16,256]{3,2,1,0:T(8,128)}) fusion(f32[16,32,16,256]{3,2,1,0:T(8,128)} %get-tuple-element.427, f32[16,32,16,256]{3,2,1,0:T(8,128)} %get-tuple-element.452, pred[16]{0:T(512)(128)(4,1)S(1)} %broadcast_compare_fusion.2, f32[16,32,16,256]{3,2,1,0:T(8,128)} %get-tuple-element.451, ...), kind=kLoop, calls=%fused_computation.3.clone.1 | loop fusion | flops 6291456 | bytes 50331664 | tf_op jit(solution)/shard_map/while/body/jit(_where)/select_n | solution.py:115
  110.5 8.0 copy.143
  119.2 13.1 %fusion.50 = (f32[16,32,16,255]{3,2,1,0:T(8,128)}, f32[16,32,16,255]{3,2,1,0:T(8,128)}) fusion(f32[16,32,16,256]{3,2,1,0:T(8,128)} %get-tuple-element.453), kind=kLoop, calls=%fused_computation.93.clone.1 | loop fusion | bytes 33423360 | tf_op jit(solution)/shard_map/while/body/slice | solution.py:79
  132.3 7.3 fusion.51
  146.5 28.9 %add_select_fusion.3 = (f32[16,32,16,256]{3,2,1,0:T(8,128)}, f32[16,32,16,256]{3,2,1,0:T(8,128)}) fusion(f32[16,32,16,256]{3,2,1,0:T(8,128)} %get-tuple-element.453, f32[16,16,256]{2,1,0:T(8,128)S(1)} %bitcast.121, f32[]{:T(128)S(6)} %div.102, f32[]{:T(128)S(6)} %mul.491, pred[16]{0:T(512)(128)(4,1)S(1)} %broadcast_compare_fusion.2, ...), kind=kLoop, calls=%fused_computation.1.clone.1 | loop fusion | flops 39845888 | bytes 83820568 | tf_op jit(solution)/shard_map/while/body/jit(_where)/select_n | solution.py:116
  175.4 19.2 %broadcast_select_fusion.8 = (f32[16,32,16,256]{3,2,1,0:T(8,128)}, f32[16,32,16,256]{3,2,1,0:T(8,128)}) fusion(f32[16,32,16,256]{3,2,1,0:T(8,128)} %get-tuple-element.427, f32[16,32,16,256]{3,2,1,0:T(8,128)} %get-tuple-element.452, pred[16]{0:T(512)(128)(4,1)S(1)} %broadcast_compare_fusion.2, f32[16,32,16,256]{3,2,1,0:T(8,128)} %get-tuple-element.451, ...), kind=kLoop, calls=%fused_computation.3.clone.1 | loop fusion | flops 6291456 | bytes 50331664 | tf_op jit(solution)/shard_map/while/body/jit(_where)/select_n | solution.py:115
  194.6 8.0 copy.143
  203.2 13.1 %fusion.50 = (f32[16,32,16,255]{3,2,1,0:T(8,128)}, f32[16,32,16,255]{3,2,1,0:T(8,128)}) fusion(f32[16,32,16,256]{3,2,1,0:T(8,128)} %get-tuple-element.453), kind=kLoop, calls=%fused_computation.93.clone.1 | loop fusion | bytes 33423360 | tf_op jit(solution)/shard_map/while/body/slice | solution.py:79
  230.5 28.9 %add_select_fusion.3 = (f32[16,32,16,256]{3,2,1,0:T(8,128)}, f32[16,32,16,256]{3,2,1,0:T(8,128)}) fusion(f32[16,32,16,256]{3,2,1,0:T(8,128)} %get-tuple-element.453, f32[16,16,256]{2,1,0:T(8,128)S(1)} %bitcast.121, f32[]{:T(128)S(6)} %div.102, f32[]{:T(128)S(6)} %mul.491, pred[16]{0:T(512)(128)(4,1)S(1)} %broadcast_compare_fusion.2, ...), kind=kLoop, calls=%fused_computation.1.clone.1 | loop fusion | flops 39845888 | bytes 83820568 | tf_op jit(solution)/shard_map/while/body/jit(_where)/select_n | solution.py:116
  259.4 19.2 %broadcast_select_fusion.8 = (f32[16,32,16,256]{3,2,1,0:T(8,128)}, f32[16,32,16,256]{3,2,1,0:T(8,128)}) fusion(f32[16,32,16,256]{3,2,1,0:T(8,128)} %get-tuple-element.427, f32[16,32,16,256]{3,2,1,0:T(8,128)} %get-tuple-element.452, pred[16]{0:T(512)(128)(4,1)S(1)} %broadcast_compare_fusion.2, f32[16,32,16,256]{3,2,1,0:T(8,128)} %get-tuple-element.451, ...), kind=kLoop, calls=%fused_computation.3.clone.1 | loop fusion | flops 6291456 | bytes 50331664 | tf_op jit(solution)/shard_map/while/body/jit(_where)/select_n | solution.py:115
  278.6 8.0 copy.143
  287.3 13.1 %fusion.50 = (f32[16,32,16,255]{3,2,1,0:T(8,128)}, f32[16,32,16,255]{3,2,1,0:T(8,128)}) fusion(f32[16,32,16,256]{3,2,1,0:T(8,128)} %get-tuple-element.453), kind=kLoop, calls=%fused_computation.93.clone.1 | loop fusion | bytes 33423360 | tf_op jit(solution)/shard_map/while/body/slice | solution.py:79
  300.5 7.3 fusion.51
  314.6 28.9 %add_select_fusion.3 = (f32[16,32,16,256]{3,2,1,0:T(8,128)}, f32[16,32,16,256]{3,2,1,0:T(8,128)}) fusion(f32[16,32,16,256]{3,2,1,0:T(8,128)} %get-tuple-element.453, f32[16,16,256]{2,1,0:T(8,128)S(1)} %bitcast.121, f32[]{:T(128)S(6)} %div.102, f32[]{:T(128)S(6)} %mul.491, pred[16]{0:T(512)(128)(4,1)S(1)} %broadcast_compare_fusion.2, ...), kind=kLoop, calls=%fused_computation.1.clone.1 | loop fusion | flops 39845888 | bytes 83820568 | tf_op jit(solution)/shard_map/while/body/jit(_where)/select_n | solution.py:116
  343.5 19.2 %broadcast_select_fusion.8 = (f32[16,32,16,256]{3,2,1,0:T(8,128)}, f32[16,32,16,256]{3,2,1,0:T(8,128)}) fusion(f32[16,32,16,256]{3,2,1,0:T(8,128)} %get-tuple-element.427, f32[16,32,16,256]{3,2,1,0:T(8,128)} %get-tuple-element.452, pred[16]{0:T(512)(128)(4,1)S(1)} %broadcast_compare_fusion.2, f32[16,32,16,256]{3,2,1,0:T(8,128)} %get-tuple-element.451, ...), kind=kLoop, calls=%fused_computation.3.clone.1 | loop fusion | flops 6291456 | bytes 50331664 | tf_op jit(solution)/shard_map/while/body/jit(_where)/select_n | solution.py:115
  362.7 8.0 copy.143
  371.4 13.1 %fusion.50 = (f32[16,32,16,255]{3,2,1,0:T(8,128)}, f32[16,32,16,255]{3,2,1,0:T(8,128)}) fusion(f32[16,32,16,256]{3,2,1,0:T(8,128)} %get-tuple-element.453), kind=kLoop, calls=%fused_computation.93.clone.1 | loop fusion | bytes 33423360 | tf_op jit(solution)/shard_map/while/body/slice | solution.py:79
  384.5 7.3 fusion.51
  398.6 28.9 %add_select_fusion.3 = (f32[16,32,16,256]{3,2,1,0:T(8,128)}, f32[16,32,16,256]{3,2,1,0:T(8,128)}) fusion(f32[16,32,16,256]{3,2,1,0:T(8,128)} %get-tuple-element.453, f32[16,16,256]{2,1,0:T(8,128)S(1)} %bitcast.121, f32[]{:T(128)S(6)} %div.102, f32[]{:T(128)S(6)} %mul.491, pred[16]{0:T(512)(128)(4,1)S(1)} %broadcast_compare_fusion.2, ...), kind=kLoop, calls=%fused_computation.1.clone.1 | loop fusion | flops 39845888 | bytes 83820568 | tf_op jit(solution)/shard_map/while/body/jit(_where)/select_n | solution.py:116
  427.6 19.2 %broadcast_select_fusion.8 = (f32[16,32,16,256]{3,2,1,0:T(8,128)}, f32[16,32,16,256]{3,2,1,0:T(8,128)}) fusion(f32[16,32,16,256]{3,2,1,0:T(8,128)} %get-tuple-element.427, f32[16,32,16,256]{3,2,1,0:T(8,128)} %get-tuple-element.452, pred[16]{0:T(512)(128)(4,1)S(1)} %broadcast_compare_fusion.2, f32[16,32,16,256]{3,2,1,0:T(8,128)} %get-tuple-element.451, ...), kind=kLoop, calls=%fused_computation.3.clone.1 | loop fusion | flops 6291456 | bytes 50331664 | tf_op jit(solution)/shard_map/while/body/jit(_where)/select_n | solution.py:115
  446.7 8.0 copy.143
  455.4 13.1 %fusion.50 = (f32[16,32,16,255]{3,2,1,0:T(8,128)}, f32[16,32,16,255]{3,2,1,0:T(8,128)}) fusion(f32[16,32,16,256]{3,2,1,0:T(8,128)} %get-tuple-element.453), kind=kLoop, calls=%fused_computation.93.clone.1 | loop fusion | bytes 33423360 | tf_op jit(solution)/shard_map/while/body/slice | solution.py:79
  482.7 28.9 %add_select_fusion.3 = (f32[16,32,16,256]{3,2,1,0:T(8,128)}, f32[16,32,16,256]{3,2,1,0:T(8,128)}) fusion(f32[16,32,16,256]{3,2,1,0:T(8,128)} %get-tuple-element.453, f32[16,16,256]{2,1,0:T(8,128)S(1)} %bitcast.121, f32[]{:T(128)S(6)} %div.102, f32[]{:T(128)S(6)} %mul.491, pred[16]{0:T(512)(128)(4,1)S(1)} %broadcast_compare_fusion.2, ...), kind=kLoop, calls=%fused_computation.1.clone.1 | loop fusion | flops 39845888 | bytes 83820568 | tf_op jit(solution)/shard_map/while/body/jit(_where)/select_n | solution.py:116
  511.6 19.2 %broadcast_select_fusion.8 = (f32[16,32,16,256]{3,2,1,0:T(8,128)}, f32[16,32,16,256]{3,2,1,0:T(8,128)}) fusion(f32[16,32,16,256]{3,2,1,0:T(8,128)} %get-tuple-element.427, f32[16,32,16,256]{3,2,1,0:T(8,128)} %get-tuple-element.452, pred[16]{0:T(512)(128)(4,1)S(1)} %broadcast_compare_fusion.2, f32[16,32,16,256]{3,2,1,0:T(8,128)} %get-tuple-element.451, ...), kind=kLoop, calls=%fused_computation.3.clone.1 | loop fusion | flops 6291456 | bytes 50331664 | tf_op jit(solution)/shard_map/while/body/jit(_where)/select_n | solution.py:115
  530.8 8.0 copy.143
  539.5 13.1 %fusion.50 = (f32[16,32,16,255]{3,2,1,0:T(8,128)}, f32[16,32,16,255]{3,2,1,0:T(8,128)}) fusion(f32[16,32,16,256]{3,2,1,0:T(8,128)} %get-tuple-element.453), kind=kLoop, calls=%fused_computation.93.clone.1 | loop fusion | bytes 33423360 | tf_op jit(solution)/shard_map/while/body/slice | solution.py:79
  552.6 7.3 fusion.51
  566.8 28.9 %add_select_fusion.3 = (f32[16,32,16,256]{3,2,1,0:T(8,128)}, f32[16,32,16,256]{3,2,1,0:T(8,128)}) fusion(f32[16,32,16,256]{3,2,1,0:T(8,128)} %get-tuple-element.453, f32[16,16,256]{2,1,0:T(8,128)S(1)} %bitcast.121, f32[]{:T(128)S(6)} %div.102, f32[]{:T(128)S(6)} %mul.491, pred[16]{0:T(512)(128)(4,1)S(1)} %broadcast_compare_fusion.2, ...), kind=kLoop, calls=%fused_computation.1.clone.1 | loop fusion | flops 39845888 | bytes 83820568 | tf_op jit(solution)/shard_map/while/body/jit(_where)/select_n | solution.py:116
  595.7 19.2 %broadcast_select_fusion.8 = (f32[16,32,16,256]{3,2,1,0:T(8,128)}, f32[16,32,16,256]{3,2,1,0:T(8,128)}) fusion(f32[16,32,16,256]{3,2,1,0:T(8,128)} %get-tuple-element.427, f32[16,32,16,256]{3,2,1,0:T(8,128)} %get-tuple-element.452, pred[16]{0:T(512)(128)(4,1)S(1)} %broadcast_compare_fusion.2, f32[16,32,16,256]{3,2,1,0:T(8,128)} %get-tuple-element.451, ...), kind=kLoop, calls=%fused_computation.3.clone.1 | loop fusion | flops 6291456 | bytes 50331664 | tf_op jit(solution)/shard_map/while/body/jit(_where)/select_n | solution.py:115
  614.9 8.0 copy.143
  623.5 13.1 %fusion.50 = (f32[16,32,16,255]{3,2,1,0:T(8,128)}, f32[16,32,16,255]{3,2,1,0:T(8,128)}) fusion(f32[16,32,16,256]{3,2,1,0:T(8,128)} %get-tuple-element.453), kind=kLoop, calls=%fused_computation.93.clone.1 | loop fusion | bytes 33423360 | tf_op jit(solution)/shard_map/while/body/slice | solution.py:79
  636.7 7.3 fusion.51
  650.8 28.9 %add_select_fusion.3 = (f32[16,32,16,256]{3,2,1,0:T(8,128)}, f32[16,32,16,256]{3,2,1,0:T(8,128)}) fusion(f32[16,32,16,256]{3,2,1,0:T(8,128)} %get-tuple-element.453, f32[16,16,256]{2,1,0:T(8,128)S(1)} %bitcast.121, f32[]{:T(128)S(6)} %div.102, f32[]{:T(128)S(6)} %mul.491, pred[16]{0:T(512)(128)(4,1)S(1)} %broadcast_compare_fusion.2, ...), kind=kLoop, calls=%fused_computation.1.clone.1 | loop fusion | flops 39845888 | bytes 83820568 | tf_op jit(solution)/shard_map/while/body/jit(_where)/select_n | solution.py:116
  679.7 19.2 %broadcast_select_fusion.8 = (f32[16,32,16,256]{3,2,1,0:T(8,128)}, f32[16,32,16,256]{3,2,1,0:T(8,128)}) fusion(f32[16,32,16,256]{3,2,1,0:T(8,128)} %get-tuple-element.427, f32[16,32,16,256]{3,2,1,0:T(8,128)} %get-tuple-element.452, pred[16]{0:T(512)(128)(4,1)S(1)} %broadcast_compare_fusion.2, f32[16,32,16,256]{3,2,1,0:T(8,128)} %get-tuple-element.451, ...), kind=kLoop, calls=%fused_computation.3.clone.1 | loop fusion | flops 6291456 | bytes 50331664 | tf_op jit(solution)/shard_map/while/body/jit(_where)/select_n | solution.py:115
  698.9 8.0 copy.143
  707.9 10.0 %copy_multiply_fusion = f32[16,32,16,256]{3,1,2,0:T(8,128)S(1)} fusion(f32[16,32,16,256]{3,2,1,0:T(8,128)} %get-tuple-element.191, f32[16,256]{1,0:T(8,128)S(1)} %fusion.32), kind=kLoop, calls=%fused_computation.5 | loop fusion | flops 2097152 | bytes 16793600 | tf_op jit(solution)/shard_map/mul | solution.py:158
  722.5 19.6 %copy.85 = f32[16,32,16,256]{1,3,2,0:T(8,128)} copy(f32[16,32,16,256]{3,1,2,0:T(8,128)} %copy-done) | data formatting | bytes 16777216 | tf_op jit(solution)/shard_map/mul | solution.py:158
  744.3 10.0 %fusion.46 = f32[16,16,4,8,256]{4,3,2,1,0:T(8,128)S(1)} fusion(f32[16,256]{1,0:T(8,128)S(1)} %fusion.32, f32[16,32,16,256]{3,2,1,0:T(8,128)} %get-tuple-element.191), kind=kLoop, calls=%fused_computation.95 | loop fusion | flops 2097152 | bytes 16793600
  755.6 8.3 %convolution_multiply_fusion = f32[16,32,32]{2,1,0:T(8,128)S(1)} fusion(f32[16,32,4096]{2,1,0:T(8,128)S(1)} %bitcast.110), kind=kOutput, calls=%fused_computation.13 | convolution fusion | flops 805322752 | bytes 8454144 | tf_op jit(solution)/shard_map/bkc,blc->bkl/dot_general | solution.py:161
  763.9 7.9 slice.126
  771.7 8.3 %slice.125 = f32[16,32,16,4,16]{1,4,3,2,0:T(8,128)} slice(f32[16,32,16,16,16]{1,4,3,2,0:T(8,128)} %bitcast.109), slice={[0:16], [0:32], [0:16], [12:16], [0:16]} | slice | bytes 4194304 | tf_op jit(solution)/shard_map/slice | solution.py:173
  785.7 15.5 %fusion.4 = f32[16,32,32]{2,1,0:T(8,128)S(1)} fusion(f32[16,32,1024]{1,2,0:T(8,128)} %bitcast.111, f32[1,32,1024]{2,1,0:T(8,128)S(1)} %bitcast.128, f32[15,32,1024]{2,1,0:T(8,128)S(1)} %copy.87), kind=kOutput, calls=%fused_computation.11 | convolution fusion | flops 201867264 | bytes 4259840 | tf_op jit(solution)/shard_map/bkc,blc->bkl/dot_general | solution.py:177
  (133 shorter events, 106.0 us)
Async XLA Ops:
  0.6 8.1 copy-start.1
  15.8 4.6 copy-start.2
  15.8 4.6 copy-start.3
  15.8 4.6 copy-start.4
  15.8 4.6 copy-start.5
  15.8 4.6 copy-start.6
  15.8 4.6 copy-start.7
  15.8 4.6 copy-start.8
  21.0 7.9 copy-start.13
  34.0 673.8 %copy-start.9 = (s32[256]{0:T(256)S(1)}, s32[256]{0:T(256)}, u32[]{:S(2)}) copy-start(s32[256]{0:T(256)} %get-tuple-element.315) | copy-start | bytes 3076
  34.0 673.8 %copy-start.10 = (s32[256]{0:T(256)S(1)}, s32[256]{0:T(256)}, u32[]{:S(2)}) copy-start(s32[256]{0:T(256)} %get-tuple-element.316) | copy-start | bytes 3076
  34.0 673.8 %copy-start.11 = (pred[256]{0:T(512)(128)(4,1)S(1)}, pred[256]{0:T(512)(128)(4,1)}, u32[]{:S(2)}) copy-start(pred[256]{0:T(512)(128)(4,1)} %compare_and_fusion) | copy-start | bytes 772
  34.0 673.8 %copy-start.12 = (f32[16]{0:T(128)S(1)}, f32[16]{0:T(128)}, u32[]{:S(2)}) copy-start(f32[16]{0:T(128)} %minimum_minimum_fusion) | copy-start | bytes 196
  35.1 13.2 %slice-start = ((s8[8388608]{0:T(1024)(128)(4,1)}), s8[4194304]{0:T(1024)(128)(4,1)S(1)}, s32[]{:S(2)}) async-start(s8[8388608]{0:T(1024)(128)(4,1)} %bitcast.104), calls=%async_computation | async-start | bytes 8388608 | tf_op jit(solution)/shard_map/while
  35.1 13.1 %slice-start.1 = ((s8[8388608]{0:T(1024)(128)(4,1)}), s8[4194304]{0:T(1024)(128)(4,1)S(1)}, s32[]{:S(2)}) async-start(s8[8388608]{0:T(1024)(128)(4,1)} %bitcast.104), calls=%async_computation.1 | async-start | bytes 8388608 | tf_op jit(solution)/shard_map/while
  119.2 13.2 %slice-start = ((s8[8388608]{0:T(1024)(128)(4,1)}), s8[4194304]{0:T(1024)(128)(4,1)S(1)}, s32[]{:S(2)}) async-start(s8[8388608]{0:T(1024)(128)(4,1)} %bitcast.104), calls=%async_computation | async-start | bytes 8388608 | tf_op jit(solution)/shard_map/while
  119.2 13.1 %slice-start.1 = ((s8[8388608]{0:T(1024)(128)(4,1)}), s8[4194304]{0:T(1024)(128)(4,1)S(1)}, s32[]{:S(2)}) async-start(s8[8388608]{0:T(1024)(128)(4,1)} %bitcast.104), calls=%async_computation.1 | async-start | bytes 8388608 | tf_op jit(solution)/shard_map/while
  203.2 13.2 %slice-start = ((s8[8388608]{0:T(1024)(128)(4,1)}), s8[4194304]{0:T(1024)(128)(4,1)S(1)}, s32[]{:S(2)}) async-start(s8[8388608]{0:T(1024)(128)(4,1)} %bitcast.104), calls=%async_computation | async-start | bytes 8388608 | tf_op jit(solution)/shard_map/while
  203.2 13.1 %slice-start.1 = ((s8[8388608]{0:T(1024)(128)(4,1)}), s8[4194304]{0:T(1024)(128)(4,1)S(1)}, s32[]{:S(2)}) async-start(s8[8388608]{0:T(1024)(128)(4,1)} %bitcast.104), calls=%async_computation.1 | async-start | bytes 8388608 | tf_op jit(solution)/shard_map/while
  287.3 13.2 %slice-start = ((s8[8388608]{0:T(1024)(128)(4,1)}), s8[4194304]{0:T(1024)(128)(4,1)S(1)}, s32[]{:S(2)}) async-start(s8[8388608]{0:T(1024)(128)(4,1)} %bitcast.104), calls=%async_computation | async-start | bytes 8388608 | tf_op jit(solution)/shard_map/while
  287.3 13.1 %slice-start.1 = ((s8[8388608]{0:T(1024)(128)(4,1)}), s8[4194304]{0:T(1024)(128)(4,1)S(1)}, s32[]{:S(2)}) async-start(s8[8388608]{0:T(1024)(128)(4,1)} %bitcast.104), calls=%async_computation.1 | async-start | bytes 8388608 | tf_op jit(solution)/shard_map/while
  371.3 13.2 %slice-start = ((s8[8388608]{0:T(1024)(128)(4,1)}), s8[4194304]{0:T(1024)(128)(4,1)S(1)}, s32[]{:S(2)}) async-start(s8[8388608]{0:T(1024)(128)(4,1)} %bitcast.104), calls=%async_computation | async-start | bytes 8388608 | tf_op jit(solution)/shard_map/while
  371.4 13.1 %slice-start.1 = ((s8[8388608]{0:T(1024)(128)(4,1)}), s8[4194304]{0:T(1024)(128)(4,1)S(1)}, s32[]{:S(2)}) async-start(s8[8388608]{0:T(1024)(128)(4,1)} %bitcast.104), calls=%async_computation.1 | async-start | bytes 8388608 | tf_op jit(solution)/shard_map/while
  455.4 13.2 %slice-start = ((s8[8388608]{0:T(1024)(128)(4,1)}), s8[4194304]{0:T(1024)(128)(4,1)S(1)}, s32[]{:S(2)}) async-start(s8[8388608]{0:T(1024)(128)(4,1)} %bitcast.104), calls=%async_computation | async-start | bytes 8388608 | tf_op jit(solution)/shard_map/while
  455.4 13.1 %slice-start.1 = ((s8[8388608]{0:T(1024)(128)(4,1)}), s8[4194304]{0:T(1024)(128)(4,1)S(1)}, s32[]{:S(2)}) async-start(s8[8388608]{0:T(1024)(128)(4,1)} %bitcast.104), calls=%async_computation.1 | async-start | bytes 8388608 | tf_op jit(solution)/shard_map/while
  539.5 13.2 %slice-start = ((s8[8388608]{0:T(1024)(128)(4,1)}), s8[4194304]{0:T(1024)(128)(4,1)S(1)}, s32[]{:S(2)}) async-start(s8[8388608]{0:T(1024)(128)(4,1)} %bitcast.104), calls=%async_computation | async-start | bytes 8388608 | tf_op jit(solution)/shard_map/while
  539.5 13.1 %slice-start.1 = ((s8[8388608]{0:T(1024)(128)(4,1)}), s8[4194304]{0:T(1024)(128)(4,1)S(1)}, s32[]{:S(2)}) async-start(s8[8388608]{0:T(1024)(128)(4,1)} %bitcast.104), calls=%async_computation.1 | async-start | bytes 8388608 | tf_op jit(solution)/shard_map/while
  623.5 13.2 %slice-start = ((s8[8388608]{0:T(1024)(128)(4,1)}), s8[4194304]{0:T(1024)(128)(4,1)S(1)}, s32[]{:S(2)}) async-start(s8[8388608]{0:T(1024)(128)(4,1)} %bitcast.104), calls=%async_computation | async-start | bytes 8388608 | tf_op jit(solution)/shard_map/while
  623.5 13.1 %slice-start.1 = ((s8[8388608]{0:T(1024)(128)(4,1)}), s8[4194304]{0:T(1024)(128)(4,1)S(1)}, s32[]{:S(2)}) async-start(s8[8388608]{0:T(1024)(128)(4,1)} %bitcast.104), calls=%async_computation.1 | async-start | bytes 8388608 | tf_op jit(solution)/shard_map/while
  717.8 3.3 copy-start
  722.5 79.5 %collective-permute-start = (f32[16,32,4,256]{3,1,2,0:T(8,128)}, f32[16,32,4,256]{3,1,2,0:T(8,128)}, u32[]{:S(2)}, u32[]{:S(2)}) collective-permute-start(f32[16,32,4,256]{3,1,2,0:T(8,128)} %slice.124), channel_id=1, source_target_pairs={{4,0},{8,4},{12,8},{16,12},{20,16},{24,20},{28,24},{32,28},{36,32}... | collective-permute-start | bytes 6291464 | tf_op jit(solution)/shard_map/ppermute | solution.py:20
  743.4 42.3 %collective-permute-start.1 = (f32[32,1024]{1,0:T(8,128)S(1)}, f32[32,1024]{1,0:T(8,128)S(1)}, u32[]{:S(2)}, u32[]{:S(2)}) collective-permute-start(f32[32,1024]{1,0:T(8,128)S(1)} %copy.86), channel_id=1, source_target_pairs={{1,0},{2,1},{3,2},{0,3},{5,4},{6,5},{7,6},{4,7},{9,8},{10,9},{11,1... | collective-permute-start | bytes 393224 | tf_op jit(solution)/shard_map/ppermute | solution.py:20
where the time goes:
time: 820 us; the launch traced here: 807 us
  other arithmetic  419 us (51%)
  local copies, waits for them, and re-layouts  351 us (43%)
  matrix products  28 us (3%)
    select_n x8, other arithmetic, sweep_step(): jnp.where(live, turned, direction)  231 us
    select_n x8, other arithmetic, sweep_step(): jnp.where(live, reduced, residual)  153 us
    slice x8, local copies, waits for them, and re-layouts, neighbours(): field[..., 1:]  105 us
    while x40, local copies, waits for them, and re-layouts  64.5 us
    slice x8, local copies, waits for them, and re-layouts, neighbours(): field[..., edge_len:]  58.1 us
    slice x8, local copies, waits for them, and re-layouts, neighbours(): field[..., 1:, :]  54.5 us
    mul x1, local copies, waits for them, and re-layouts, on_device(): weighted = snapshot * partition(edge_len)  19.6 us
  transfers between devices with their start and end apart: 2, of which 0 were waited for; matrix products, arithmetic and copies ran while one was open for 10% of the time, Pallas kernels for 0%

commit v1 on v0

v1 whole, which is shorter than its diff:
```python
import functools

import numpy as np
import jax
import jax.numpy as jnp
from jax import lax
from jax.experimental import pallas as pl
from jax.experimental.pallas import tpu as pltpu
from jax.sharding import PartitionSpec as P

MARGIN = 4
MAX_SWEEPS = 8

REACTION = 1.0
BOUND_LOW = 0.1
BOUND_HIGH = 2.0
CENTRE = 0.5 * (BOUND_LOW + BOUND_HIGH)
HALF_WIDTH = 0.5 * (BOUND_HIGH - BOUND_LOW)
SIGMA_RATIO = CENTRE / HALF_WIDTH

HIGHEST = lax.Precision.HIGHEST


def sweep_constants():
    rho = np.float32(1.0 / SIGMA_RATIO)
    two_sigma = np.float32(2.0 * SIGMA_RATIO)
    pairs = []
    for _ in range(MAX_SWEEPS):
        rho_next = np.float32(np.float32(1.0) / np.float32(two_sigma - rho))
        keep = np.float32(rho_next * rho)
        push = np.float32(np.float32(np.float32(2.0) * rho_next) / np.float32(HALF_WIDTH))
        pairs.append((float(keep), float(push)))
        rho = rho_next
    return pairs


def from_behind(block, axis, distance):
    devices = range(lax.axis_size(axis))
    route = [((i - distance) % len(devices), i) for i in devices]
    return lax.ppermute(block, axis, route)


def prepare(coefficient):
    edge_len = coefficient.shape[-2]
    plane_len = coefficient.shape[-1]
    x_index = lax.broadcasted_iota(jnp.int32, (edge_len, plane_len), 0)
    flat_index = lax.broadcasted_iota(jnp.int32, (edge_len, plane_len), 1)
    y_index = flat_index // edge_len
    z_index = flat_index % edge_len
    x_next = jnp.concatenate([coefficient[..., 1:, :], coefficient[..., -1:, :]], axis=-2)
    x_prev = jnp.concatenate([coefficient[..., :1, :], coefficient[..., :-1, :]], axis=-2)
    y_next = jnp.concatenate([coefficient[..., edge_len:], coefficient[..., -edge_len:]], axis=-1)
    y_prev = jnp.concatenate([coefficient[..., :edge_len], coefficient[..., :-edge_len]], axis=-1)
    z_next = jnp.where(
        z_index == edge_len - 1,
        coefficient,
        jnp.concatenate([coefficient[..., 1:], coefficient[..., -1:]], axis=-1),
    )
    z_prev = jnp.where(
        z_index == 0,
        coefficient,
        jnp.concatenate([coefficient[..., :1], coefficient[..., :-1]], axis=-1),
    )
    faces = (
        (coefficient + x_next) * 0.5,
        (coefficient + x_prev) * 0.5,
        (coefficient + y_next) * 0.5,
        (coefficient + y_prev) * 0.5,
        (coefficient + z_next) * 0.5,
        (coefficient + z_prev) * 0.5,
    )
    diagonal = REACTION + faces[0]
    for face in faces[1:]:
        diagonal = diagonal + face
    keeps = (
        x_index < edge_len - 1,
        x_index > 0,
        y_index < edge_len - 1,
        y_index > 0,
        z_index < edge_len - 1,
        z_index > 0,
    )
    off_terms = tuple(
        (jnp.where(keep, face, jnp.zeros_like(face)) for keep, face in zip(keeps, faces))
    )
    return (diagonal, off_terms)


def ramp(position, edge_len):
    return jnp.minimum(
        1.0, jnp.minimum((position + 0.5) / MARGIN, (edge_len - position - 0.5) / MARGIN)
    )


def partition(edge_len):
    x_index = lax.broadcasted_iota(jnp.int32, (edge_len, edge_len * edge_len), 0)
    flat_index = lax.broadcasted_iota(jnp.int32, (edge_len, edge_len * edge_len), 1)
    x_float = x_index.astype(jnp.float32)
    y_float = (flat_index // edge_len).astype(jnp.float32)
    return ramp(x_float, edge_len) * ramp(y_float, edge_len)


def gram(a, b):
    return lax.dot_general(
        a, b, (((1,), (1,)), ((), ())), precision=HIGHEST, preferred_element_type=jnp.float32
    )


def brick_kernel(
    counts_ref, force_lo, force_hi, terms_ref, blend_ref,
    self_ref, up_ref, lo_ref, col_ref, front_ref, back_ref,
    snap, resid, direc, terms, behind,
    *, edge_len, columns,
):
    b = pl.program_id(0)
    last = pl.num_programs(0) - 1
    count = counts_ref[b]
    groups = columns // 8
    plane = edge_len * edge_len
    scale_pair = float((MARGIN * edge_len * edge_len) ** (-0.5))

    def rep(row):
        return jnp.concatenate([row] * groups, axis=0)

    for k in range(8):
        for x in range(edge_len):
            terms[k, x] = jnp.broadcast_to(terms_ref[k, x : x + 1, :], (8, plane))

    start_scale = float(np.float32(1.0 / CENTRE))
    for x in range(edge_len):
        rows = pl.ds(x, columns, stride=edge_len)
        f = jnp.concatenate([force_lo[rows, :], force_hi[rows, :]], axis=1)
        resid[x] = f
        direc[0, x] = f * rep(terms[7, x]) * start_scale
        snap[x] = jnp.zeros_like(f)

    for t, (keep, push) in enumerate(sweep_constants()):
        src, dst = t % 2, (t + 1) % 2

        @pl.when(t < count)
        def _():
            def one_plane(x, carry):
                xm = jnp.maximum(x - 1, 0)
                xp = jnp.minimum(x + 1, edge_len - 1)
                d0 = direc[src, x]
                res = rep(terms[0, x]) * d0
                res = res - rep(terms[1, x]) * direc[src, xp]
                res = res - rep(terms[2, x]) * direc[src, xm]
                res = res - rep(terms[3, x]) * pltpu.roll(d0, plane - edge_len, 1)
                res = res - rep(terms[4, x]) * pltpu.roll(d0, edge_len, 1)
                res = res - rep(terms[5, x]) * pltpu.roll(d0, plane - 1, 1)
                res = res - rep(terms[6, x]) * pltpu.roll(d0, 1, 1)
                r = resid[x] - res
                resid[x] = r
                snap[x] = snap[x] + d0
                direc[dst, x] = keep * d0 + push * (r * rep(terms[7, x]))
                return carry

            lax.fori_loop(0, edge_len, one_plane, 0)

    lane = lax.broadcasted_iota(jnp.int32, (columns, plane), 1)
    front_lanes = lane < MARGIN * edge_len

    def finish(x, acc):
        g, c = acc
        w = snap[x] * jnp.broadcast_to(blend_ref[pl.ds(x, 1), :], (columns, plane))
        snap[x] = w
        g = g + gram(w, w)
        front = jnp.where(front_lanes, w, 0.0)
        c = c + gram(behind[x], front)
        behind[x] = jnp.where(front_lanes, pltpu.roll(w, MARGIN * edge_len, 1), 0.0)
        return g, c

    zero = jnp.zeros((columns, columns), jnp.float32)
    g, c = lax.fori_loop(0, edge_len, finish, (zero, zero))
    self_ref[...] = g / float(edge_len**3)

    @pl.when(b > 0)
    def _():
        col_ref[b - 1] = c * scale_pair

    for a in range(MARGIN):
        up_ref[a] = snap[a]
        lo_ref[a] = snap[edge_len - MARGIN + a]

    @pl.when(b == 0)
    def _():
        for x in range(edge_len):
            front_ref[x] = jnp.where(front_lanes, snap[x], 0.0)

    @pl.when(b == last)
    def _():
        for x in range(edge_len):
            back_ref[x] = behind[x]


def run_bricks(force, coefficient, counts):
    bricks, columns, edge_len, plane = force.shape
    diagonal, off_terms = prepare(coefficient)
    inverse = 1.0 / diagonal
    terms_in = jnp.stack((diagonal,) + off_terms + (inverse,), axis=1)
    blend = partition(edge_len)
    force2 = force.reshape(bricks, columns * edge_len, plane)
    kernel = functools.partial(brick_kernel, edge_len=edge_len, columns=columns)
    f32 = jnp.float32
    out_shape = (
        jax.ShapeDtypeStruct((bricks, columns, columns), f32),
        jax.ShapeDtypeStruct((bricks, MARGIN, columns, plane), f32),
        jax.ShapeDtypeStruct((bricks, MARGIN, columns, plane), f32),
        jax.ShapeDtypeStruct((bricks, columns, columns), f32),
        jax.ShapeDtypeStruct((edge_len, columns, plane), f32),
        jax.ShapeDtypeStruct((edge_len, columns, plane), f32),
    )
    grid_spec = pltpu.PrefetchScalarGridSpec(
        num_scalar_prefetch=1,
        grid=(bricks,),
        in_specs=[
            pl.BlockSpec((None, columns * edge_len, 128), lambda b, c: (b, 0, 0)),
            pl.BlockSpec((None, columns * edge_len, 128), lambda b, c: (b, 0, 1)),
            pl.BlockSpec((None, 8, edge_len, plane), lambda b, c: (b, 0, 0, 0)),
            pl.BlockSpec((edge_len, plane), lambda b, c: (0, 0)),
        ],
        out_specs=[
            pl.BlockSpec((None, columns, columns), lambda b, c: (b, 0, 0)),
            pl.BlockSpec((None, MARGIN, columns, plane), lambda b, c: (b, 0, 0, 0)),
            pl.BlockSpec((None, MARGIN, columns, plane), lambda b, c: (b, 0, 0, 0)),
            pl.BlockSpec((bricks, columns, columns), lambda b, c: (0, 0, 0)),
            pl.BlockSpec((edge_len, columns, plane), lambda b, c: (0, 0, 0)),
            pl.BlockSpec((edge_len, columns, plane), lambda b, c: (0, 0, 0)),
        ],
        scratch_shapes=[
            pltpu.VMEM((edge_len, columns, plane), f32),
            pltpu.VMEM((edge_len, columns, plane), f32),
            pltpu.VMEM((2, edge_len, columns, plane), f32),
            pltpu.VMEM((8, edge_len, 8, plane), f32),
            pltpu.VMEM((edge_len, columns, plane), f32),
        ],
    )
    return pl.pallas_call(
        kernel,
        grid_spec=grid_spec,
        out_shape=out_shape,
        compiler_params=pltpu.CompilerParams(dimension_semantics=("arbitrary",)),
    )(counts, force2, force2, terms_in, blend)


def on_device(force_columns, coefficient, sweep_counts):
    bricks = force_columns.shape[1]
    columns = force_columns.shape[2]
    edge_len = force_columns.shape[3]
    scale_pair = (MARGIN * edge_len * edge_len) ** (-0.5)
    self_part, upper, lower, col_part, front, back = run_bricks(
        force_columns[0], coefficient[0], sweep_counts[0]
    )
    below = from_behind(upper, "wide", -1)
    row_part = (
        jnp.einsum("bakc,balc->bkl", lower, below, precision=HIGHEST) * scale_pair
    )
    arrived = from_behind(front, "narrow", -1)
    last_col = jnp.einsum("xkc,xlc->kl", back, arrived, precision=HIGHEST) * scale_pair
    col_part = jnp.concatenate([col_part[:-1], last_col[None]], axis=0)
    return (
        self_part.reshape(1, bricks, -1),
        row_part.reshape(1, bricks, -1),
        col_part.reshape(1, bricks, -1),
    )


def solution(mesh):
    in_specs = (
        P("wide", "narrow", None, None, None),
        P("wide", "narrow", None, None),
        P("wide", "narrow"),
    )
    out_specs = (P("wide", "narrow", None), P("wide", "narrow", None), P("wide", "narrow", None))
    return jax.shard_map(
        on_device, mesh=mesh, in_specs=in_specs, out_specs=out_specs, check_vma=False
    )
```

time: 820 us -> 228 us (0.28); the launches traced: 807 us -> 228 us
  other arithmetic: 419 us -> 2.46 us
  local copies, waits for them, and re-layouts: 351 us -> 9.52 us
  Pallas kernels: 0 us -> 104 us
  waiting for transfers between devices: 0.01 us -> 66.9 us
  starting transfers between devices: 0.94 us -> 38.9 us
  matrix products: 28 us -> 5.21 us
    select_n x17 -> x0, other arithmetic: 386 us -> none  [the longest x8 231 us: sweep_step(): jnp.where(live, turned, direction)]
    slice x32 -> x1, local copies, waits for them, and re-layouts: 242 us -> 0.96 us  [on_device(): col_part = jnp.concatenate([col_part[:-1], last_col[None]], axis=0)]
    pallas_call x0 -> x1, Pallas kernels: none -> 104 us  [run_bricks(): pl.pallas_call(kernel, grid_spec=grid_spec, out_shape=out_shape, compiler...]
    ppermute x2, waiting for transfers between devices: 0.01 us -> 66.9 us  [from_behind(): return lax.ppermute(block, axis, route)]
    while x48 -> x0, local copies, waits for them, and re-layouts: 65.7 us -> none
    ppermute x2, starting transfers between devices: 0.94 us -> 38.9 us  [from_behind(): return lax.ppermute(block, axis, route)]
    dot_general x3 -> x2, matrix products: 28 us -> 5.21 us  [the longest x1 3.61 us: on_device(): jnp.einsum('bakc,balc->bkl', lower, below, precision=HIGHEST) * scale_pair]
    mul x1 -> x0, local copies, waits for them, and re-layouts: 19.6 us -> none  [on_device(): weighted = snapshot * partition(edge_len)]
  transfers between devices with their start and end apart: 2 -> 2, of which waited for: 0 -> 2; matrix products, arithmetic and copies ran while one was open for 10% -> 2% of each run, Pallas kernels for 0% -> 0%
where the time goes in v1:
time: 228 us
  Pallas kernels  104 us (46%)
  waiting for transfers between devices  66.9 us (29%)
  starting transfers between devices  38.9 us (17%)
  local copies, waits for them, and re-layouts  9.52 us (4%)
  matrix products  5.21 us (2%)
  other arithmetic  2.46 us (1%)
    pallas_call x1, Pallas kernels, run_bricks(): pl.pallas_call(kernel, grid_spec=grid_spec, out_shape=out_shape, compiler...  104 us
    ppermute x2, waiting for transfers between devices, from_behind(): return lax.ppermute(block, axis, route)  66.9 us
    ppermute x2, starting transfers between devices, from_behind(): return lax.ppermute(block, axis, route)  38.9 us
  transfers between devices with their start and end apart: 2, of which 2 were waited for; matrix products, arithmetic and copies ran while one was open for 2% of the time, Pallas kernels for 0%

profile of v1, /device:TPU:27, one launch (start us, length us, event | category | flops | bytes accessed | tf_op | source)
XLA Modules:
  0.0 227.7 jit_solution(12909311554493063404)
XLA Ops:
  0.6 0.0 copy-start
  0.7 1.0 slice_bitcast_fusion.11
  1.7 1.1 slice_bitcast_fusion.9
  2.8 1.1 slice_bitcast_fusion.7
  3.9 1.2 slice_bitcast_fusion.3
  5.1 0.0 copy-done
  5.1 0.1 slice_bitcast_fusion.1
  5.3 0.7 fusion.22.blend_ref
  6.0 0.4 constant_dynamic-update-slice_fusion
  6.3 0.1 bitcast_dynamic-update-slice_fusion
  6.4 0.1 select_dynamic-update-slice_fusion.4
  6.5 0.1 select_dynamic-update-slice_fusion.3
  6.6 0.1 select_dynamic-update-slice_fusion.2
  6.8 0.1 select_dynamic-update-slice_fusion.1
  6.9 0.1 select_dynamic-update-slice_fusion
  7.1 0.0 copy-start.1
  7.1 1.3 copy-done.1
  8.5 103.8 %shard_map.58 = (f32[16,32,32]{2,1,0:T(8,128)}, f32[16,4,32,256]{3,2,1,0:T(8,128)}, f32[16,4,32,256]{3,2,1,0:T(8,128)}, f32[16,32,32]{2,1,0:T(8,128)}, f32[16,32,256]{2,1,0:T(8,128)}, /*index=5*/f32[16,32,256]{2,1,0:T(8,128)}) custom-call(s32[16]{0:T(128)} %bitcast.149, f32[16,512,256]{2,1,0:T(8,128)} %bitcast.147, f32[16,512,256]{2,1,0:T(8,128)} %bitcast.148, ...), custom_call_target="tpu_custom_call" | custom-call | tf_op jit(solution)/shard_map/pallas_call | solution.py:239
  112.3 0.0 copy-start.2
  112.3 38.9 %collective-permute-start = (f32[16,4,32,256]{3,2,1,0:T(8,128)}, f32[16,4,32,256]{3,2,1,0:T(8,128)}, u32[]{:S(2)}, u32[]{:S(2)}) collective-permute-start(f32[16,4,32,256]{3,2,1,0:T(8,128)} %get-tuple-element.11), channel_id=1, source_target_pairs={{4,0},{8,4},{12,8},{16,12},{20,16},{24,20},{28,24},{32,28},{36,32}... | collective-permute-start | bytes 6291464 | tf_op jit(solution)/shard_map/ppermute | solution.py:40
  151.2 0.0 collective-permute-start.1
  151.2 1.7 reshape.453
  153.0 1.0 slice.51
  153.9 0.1 concatenate.158
  154.1 50.9 %collective-permute-done.1 = f32[16,32,256]{2,1,0:T(8,128)S(1)} collective-permute-done((f32[16,32,256]{2,1,0:T(8,128)}, f32[16,32,256]{2,1,0:T(8,128)S(1)}, u32[]{:S(2)}, u32[]{:S(2)}) %collective-permute-start.1) | collective-permute-done | bytes 524320 | tf_op jit(solution)/shard_map/ppermute | solution.py:40
  205.0 1.6 fusion.1
  206.6 0.1 concatenate.159
  206.7 0.6 pad_maximum_fusion
  207.3 16.0 %collective-permute-done = f32[16,4,32,256]{3,2,1,0:T(8,128)} collective-permute-done((f32[16,4,32,256]{3,2,1,0:T(8,128)}, f32[16,4,32,256]{3,2,1,0:T(8,128)}, u32[]{:S(2)}, u32[]{:S(2)}) %collective-permute-start) | collective-permute-done | bytes 2097184 | tf_op jit(solution)/shard_map/ppermute | solution.py:40
  223.3 0.0 copy-done.2
  223.3 3.6 %fusion = f32[16,32,32]{2,1,0:T(8,128)S(1)} fusion(f32[16,4,32,256]{3,2,1,0:T(8,128)S(1)} %copy-done.2, f32[16,4,32,256]{3,2,1,0:T(8,128)} %collective-permute-done), kind=kOutput, calls=%fused_computation.1 | convolution fusion | flops 201342976 | bytes 4259840 | tf_op jit(solution)/shard_map/bakc,balc->bkl/dot_general | solution.py:257
  226.9 0.8 reshape.454
  (11 shorter events, 0.1 us)
Async XLA Ops:
  0.6 4.4 %copy-start = (f32[1,16,16,256]{3,2,1,0:T(8,128)S(1)}, f32[1,16,16,256]{3,2,1,0:T(8,128)}, u32[]{:S(2)}) copy-start(f32[1,16,16,256]{3,2,1,0:T(8,128)} %param.4) | copy-start | bytes 786436
  7.1 1.4 copy-start.1
  112.3 111.0 %copy-start.2 = (f32[16,4,32,256]{3,2,1,0:T(8,128)S(1)}, f32[16,4,32,256]{3,2,1,0:T(8,128)}, u32[]{:S(2)}) copy-start(f32[16,4,32,256]{3,2,1,0:T(8,128)} %get-tuple-element.10) | copy-start | bytes 6291460
  112.3 111.0 %collective-permute-start = (f32[16,4,32,256]{3,2,1,0:T(8,128)}, f32[16,4,32,256]{3,2,1,0:T(8,128)}, u32[]{:S(2)}, u32[]{:S(2)}) collective-permute-start(f32[16,4,32,256]{3,2,1,0:T(8,128)} %get-tuple-element.11), channel_id=1, source_target_pairs={{4,0},{8,4},{12,8},{16,12},{20,16},{24,20},{28,24},{32,28},{36,32}... | collective-permute-start | bytes 6291464 | tf_op jit(solution)/shard_map/ppermute | solution.py:40
  151.2 53.8 %collective-permute-start.1 = (f32[16,32,256]{2,1,0:T(8,128)}, f32[16,32,256]{2,1,0:T(8,128)S(1)}, u32[]{:S(2)}, u32[]{:S(2)}) collective-permute-start(f32[16,32,256]{2,1,0:T(8,128)} %get-tuple-element.14), channel_id=1, source_target_pairs={{1,0},{2,1},{3,2},{0,3},{5,4},{6,5},{7,6},{4,7},{9,8},{10,9},{11,1... | collective-permute-start | bytes 1572872 | tf_op jit(solution)/shard_map/ppermute | solution.py:40

commit v2 on v1

--- a/solution.py
+++ b/solution.py
@@ -107,16 +107,17 @@
 
 
 def brick_kernel(
-    counts_ref, force_lo, force_hi, terms_ref, blend_ref,
+    counts_ref, consts_ref, force_lo, force_hi, terms_ref, blend_ref,
     self_ref, up_ref, lo_ref, col_ref, front_ref, back_ref,
     snap, resid, direc, terms, behind,
     *, edge_len, columns,
 ):
     b = pl.program_id(0)
     last = pl.num_programs(0) - 1
-    count = counts_ref[b]
+    count = jnp.minimum(counts_ref[b], MAX_SWEEPS)
     groups = columns // 8
     plane = edge_len * edge_len
+    band = MARGIN * edge_len
     scale_pair = float((MARGIN * edge_len * edge_len) ** (-0.5))
 
     def rep(row):
@@ -131,67 +132,71 @@
         rows = pl.ds(x, columns, stride=edge_len)
         f = jnp.concatenate([force_lo[rows, :], force_hi[rows, :]], axis=1)
         resid[x] = f
-        direc[0, x] = f * rep(terms[7, x]) * start_scale
+        direc[x] = f * rep(terms[7, x]) * start_scale
         snap[x] = jnp.zeros_like(f)
 
-    for t, (keep, push) in enumerate(sweep_constants()):
-        src, dst = t % 2, (t + 1) % 2
-
-        @pl.when(t < count)
-        def _():
-            def one_plane(x, carry):
-                xm = jnp.maximum(x - 1, 0)
-                xp = jnp.minimum(x + 1, edge_len - 1)
-                d0 = direc[src, x]
-                res = rep(terms[0, x]) * d0
-                res = res - rep(terms[1, x]) * direc[src, xp]
-                res = res - rep(terms[2, x]) * direc[src, xm]
-                res = res - rep(terms[3, x]) * pltpu.roll(d0, plane - edge_len, 1)
-                res = res - rep(terms[4, x]) * pltpu.roll(d0, edge_len, 1)
-                res = res - rep(terms[5, x]) * pltpu.roll(d0, plane - 1, 1)
-                res = res - rep(terms[6, x]) * pltpu.roll(d0, 1, 1)
-                r = resid[x] - res
-                resid[x] = r
-                snap[x] = snap[x] + d0
-                direc[dst, x] = keep * d0 + push * (r * rep(terms[7, x]))
-                return carry
-
-            lax.fori_loop(0, edge_len, one_plane, 0)
+    def sweep(t, carry):
+        keep = consts_ref[0, t]
+        push = consts_ref[1, t]
+        prev = None
+        cur = direc[0]
+        for x in range(edge_len):
+            nxt = direc[x + 1] if x + 1 < edge_len else None
+            res = rep(terms[0, x]) * cur
+            if nxt is not None:
+                res = res - rep(terms[1, x]) * nxt
+            if prev is not None:
+                res = res - rep(terms[2, x]) * prev
+            res = res - rep(terms[3, x]) * pltpu.roll(cur, plane - edge_len, 1)
+            res = res - rep(terms[4, x]) * pltpu.roll(cur, edge_len, 1)
+            res = res - rep(terms[5, x]) * pltpu.roll(cur, plane - 1, 1)
+            res = res - rep(terms[6, x]) * pltpu.roll(cur, 1, 1)
+            r = resid[x] - res
+            resid[x] = r
+            snap[x] = snap[x] + cur
+            direc[x] = keep * cur + push * (r * rep(terms[7, x]))
+            prev, cur = cur, nxt
+        return carry
+
+    lax.fori_loop(0, count, sweep, 0)
 
     lane = lax.broadcasted_iota(jnp.int32, (columns, plane), 1)
-    front_lanes = lane < MARGIN * edge_len
-
-    def finish(x, acc):
-        g, c = acc
-        w = snap[x] * jnp.broadcast_to(blend_ref[pl.ds(x, 1), :], (columns, plane))
-        snap[x] = w
-        g = g + gram(w, w)
-        front = jnp.where(front_lanes, w, 0.0)
-        c = c + gram(behind[x], front)
-        behind[x] = jnp.where(front_lanes, pltpu.roll(w, MARGIN * edge_len, 1), 0.0)
-        return g, c
-
-    zero = jnp.zeros((columns, columns), jnp.float32)
-    g, c = lax.fori_loop(0, edge_len, finish, (zero, zero))
-    self_ref[...] = g / float(edge_len**3)
+    quarter = [(lane >= band * j) & (lane < band * (j + 1)) for j in range(4)]
+    weighted = []
+    for x in range(edge_len):
+        w = snap[x] * jnp.broadcast_to(blend_ref[x : x + 1, :], (columns, plane))
+        weighted.append(w)
+    fronts, backs = [], []
+    for i in range(edge_len // 4):
+        ws = weighted[4 * i : 4 * i + 4]
+        f = jnp.where(quarter[0], ws[0], 0.0)
+        k = jnp.where(quarter[3], ws[3], 0.0)
+        for j in range(1, 4):
+            f = jnp.where(quarter[j], pltpu.roll(ws[j], band * j, 1), f)
+        for j in range(3):
+            k = jnp.where(quarter[j], pltpu.roll(ws[j], band * (j + 1), 1), k)
+        fronts.append(f)
+        backs.append(k)
+    front = jnp.concatenate(fronts, axis=1)
+    back = jnp.concatenate(backs, axis=1)
+    whole = jnp.concatenate(weighted, axis=1)
+    self_ref[...] = gram(whole, whole) / float(edge_len**3)
+    up_ref[...] = jnp.concatenate(weighted[:MARGIN], axis=1)
+    lo_ref[...] = jnp.concatenate(weighted[edge_len - MARGIN :], axis=1)
 
     @pl.when(b > 0)
     def _():
-        col_ref[b - 1] = c * scale_pair
-
-    for a in range(MARGIN):
-        up_ref[a] = snap[a]
-        lo_ref[a] = snap[edge_len - MARGIN + a]
+        col_ref[b - 1] = gram(behind[...], front) * scale_pair
+
+    behind[...] = back
 
     @pl.when(b == 0)
     def _():
-        for x in range(edge_len):
-            front_ref[x] = jnp.where(front_lanes, snap[x], 0.0)
+        front_ref[...] = front
 
     @pl.when(b == last)
     def _():
-        for x in range(edge_len):
-            back_ref[x] = behind[x]
+        back_ref[...] = back
 
 
 def run_bricks(force, coefficient, counts):
@@ -200,21 +205,25 @@
     inverse = 1.0 / diagonal
     terms_in = jnp.stack((diagonal,) + off_terms + (inverse,), axis=1)
     blend = partition(edge_len)
+    consts = jnp.asarray(np.array(sweep_constants(), np.float32).T)
     force2 = force.reshape(bricks, columns * edge_len, plane)
     kernel = functools.partial(brick_kernel, edge_len=edge_len, columns=columns)
     f32 = jnp.float32
+    slab = MARGIN * plane
+    band = plane * (edge_len // 4)
     out_shape = (
         jax.ShapeDtypeStruct((bricks, columns, columns), f32),
-        jax.ShapeDtypeStruct((bricks, MARGIN, columns, plane), f32),
-        jax.ShapeDtypeStruct((bricks, MARGIN, columns, plane), f32),
+        jax.ShapeDtypeStruct((bricks, columns, slab), f32),
+        jax.ShapeDtypeStruct((bricks, columns, slab), f32),
         jax.ShapeDtypeStruct((bricks, columns, columns), f32),
-        jax.ShapeDtypeStruct((edge_len, columns, plane), f32),
-        jax.ShapeDtypeStruct((edge_len, columns, plane), f32),
+        jax.ShapeDtypeStruct((columns, band), f32),
+        jax.ShapeDtypeStruct((columns, band), f32),
     )
     grid_spec = pltpu.PrefetchScalarGridSpec(
         num_scalar_prefetch=1,
         grid=(bricks,),
         in_specs=[
+            pl.BlockSpec(memory_space=pltpu.SMEM),
             pl.BlockSpec((None, columns * edge_len, 128), lambda b, c: (b, 0, 0)),
             pl.BlockSpec((None, columns * edge_len, 128), lambda b, c: (b, 0, 1)),
             pl.BlockSpec((None, 8, edge_len, plane), lambda b, c: (b, 0, 0, 0)),
@@ -222,18 +231,18 @@
         ],
         out_specs=[
             pl.BlockSpec((None, columns, columns), lambda b, c: (b, 0, 0)),
-            pl.BlockSpec((None, MARGIN, columns, plane), lambda b, c: (b, 0, 0, 0)),
-            pl.BlockSpec((None, MARGIN, columns, plane), lambda b, c: (b, 0, 0, 0)),
+            pl.BlockSpec((None, columns, slab), lambda b, c: (b, 0, 0)),
+            pl.BlockSpec((None, columns, slab), lambda b, c: (b, 0, 0)),
             pl.BlockSpec((bricks, columns, columns), lambda b, c: (0, 0, 0)),
-            pl.BlockSpec((edge_len, columns, plane), lambda b, c: (0, 0, 0)),
-            pl.BlockSpec((edge_len, columns, plane), lambda b, c: (0, 0, 0)),
+            pl.BlockSpec((columns, band), lambda b, c: (0, 0)),
+            pl.BlockSpec((columns, band), lambda b, c: (0, 0)),
         ],
         scratch_shapes=[
             pltpu.VMEM((edge_len, columns, plane), f32),
             pltpu.VMEM((edge_len, columns, plane), f32),
-            pltpu.VMEM((2, edge_len, columns, plane), f32),
+            pltpu.VMEM((edge_len, columns, plane), f32),
             pltpu.VMEM((8, edge_len, 8, plane), f32),
-            pltpu.VMEM((edge_len, columns, plane), f32),
+            pltpu.VMEM((columns, band), f32),
         ],
     )
     return pl.pallas_call(
@@ -241,7 +250,7 @@
         grid_spec=grid_spec,
         out_shape=out_shape,
         compiler_params=pltpu.CompilerParams(dimension_semantics=("arbitrary",)),
-    )(counts, force2, force2, terms_in, blend)
+    )(counts, consts, force2, force2, terms_in, blend)
 
 
 def on_device(force_columns, coefficient, sweep_counts):
@@ -253,11 +262,9 @@
         force_columns[0], coefficient[0], sweep_counts[0]
     )
     below = from_behind(upper, "wide", -1)
-    row_part = (
-        jnp.einsum("bakc,balc->bkl", lower, below, precision=HIGHEST) * scale_pair
-    )
+    row_part = jnp.einsum("bkc,blc->bkl", lower, below, precision=HIGHEST) * scale_pair
     arrived = from_behind(front, "narrow", -1)
-    last_col = jnp.einsum("xkc,xlc->kl", back, arrived, precision=HIGHEST) * scale_pair
+    last_col = gram(back, arrived) * scale_pair
     col_part = jnp.concatenate([col_part[:-1], last_col[None]], axis=0)
     return (
         self_part.reshape(1, bricks, -1),

time: 228 us -> 114 us (0.50)
  the two profiles are of different devices: /device:TPU:27 before, /device:TPU:12 now
where the time goes in v2:
time: 114 us
  waiting for transfers between devices  54 us (47%)
  Pallas kernels  36.4 us (32%)
  local copies, waits for them, and re-layouts  9.46 us (8%)
  starting transfers between devices  5.74 us (5%)
  matrix products  4.76 us (4%)
  other arithmetic  2.48 us (2%)
    ppermute x2, waiting for transfers between devices, from_behind(): return lax.ppermute(block, axis, route)  54 us
    pallas_call x1, Pallas kernels, run_bricks(): pl.pallas_call(kernel, grid_spec=grid_spec, out_shape=out_shape, compiler...  36.4 us
    ppermute x2, starting transfers between devices, from_behind(): return lax.ppermute(block, axis, route)  5.74 us
    dot_general x1, matrix products, on_device(): jnp.einsum('bkc,blc->bkl', lower, below, precision=HIGHEST) * scale_pair  3.6 us
  transfers between devices with their start and end apart: 2, of which 2 were waited for; matrix products, arithmetic and copies ran while one was open for 4% of the time, Pallas kernels for 0%

profile of v2, /device:TPU:12, one launch (start us, length us, event | category | flops | bytes accessed | tf_op | source)
XLA Modules:
  0.0 113.6 jit_solution(5875985828603806640)
XLA Ops:
  0.6 0.0 copy-start
  0.7 1.0 slice_bitcast_fusion.11
  1.7 1.1 slice_bitcast_fusion.9
  2.8 1.1 slice_bitcast_fusion.7
  3.9 1.2 %slice_bitcast_fusion.3 = (f32[16,1,16,240]{3,2,0,1:T(8,128)S(1)}, f32[16,1,16,240]{3,2,0,1:T(8,128)S(1)}) fusion(f32[16,16,256]{2,1,0:T(8,128)} %bitcast.135), kind=kLoop, calls=%fused_computation.11 | loop fusion | bytes 983040 | tf_op jit(solution)/shard_map/concatenate | solution.py:52
  5.0 0.0 copy-done
  5.0 0.1 slice_bitcast_fusion.1
  5.2 0.7 fusion.20.blend_ref
  5.9 0.4 constant_dynamic-update-slice_fusion
  6.3 0.1 bitcast_dynamic-update-slice_fusion
  6.4 0.1 select_dynamic-update-slice_fusion.4
  6.5 0.1 select_dynamic-update-slice_fusion.3
  6.6 0.1 select_dynamic-update-slice_fusion.2
  6.8 0.1 select_dynamic-update-slice_fusion.1
  6.9 0.1 select_dynamic-update-slice_fusion
  7.1 0.0 copy-start.1
  7.1 1.3 %copy-done.1 = f32[16,8,16,256]{3,2,1,0:T(8,128)} copy-done((f32[16,8,16,256]{3,2,1,0:T(8,128)}, f32[16,8,16,256]{3,2,1,0:T(8,128)S(1)}, u32[]{:S(2)}) %copy-start.1) | copy-done | bytes 2097176
  8.4 36.4 %shard_map.67 = (f32[16,32,32]{2,1,0:T(8,128)}, f32[16,32,1024]{2,1,0:T(8,128)}, f32[16,32,1024]{2,1,0:T(8,128)}, f32[16,32,32]{2,1,0:T(8,128)}, f32[32,1024]{1,0:T(8,128)}, /*index=5*/f32[32,1024]{1,0:T(8,128)}) custom-call(s32[16]{0:T(128)} %bitcast.140, f32[2,8]{1,0:T(2,128)} %constant.60.clone.consts_ref, f32[16,512,256]{2,1,0:T(8,128)} %bitcast.138, ...), custom_call_target="tpu_custom_call" | custom-call | tf_op jit(solution)/shard_map/pallas_call | solution.py:248
  44.8 4.6 %collective-permute-start = (f32[16,32,1024]{2,1,0:T(8,128)}, f32[16,32,1024]{2,1,0:T(8,128)S(1)}, u32[]{:S(2)}, u32[]{:S(2)}) collective-permute-start(f32[16,32,1024]{2,1,0:T(8,128)} %get-tuple-element.11), channel_id=1, source_target_pairs={{4,0},{8,4},{12,8},{16,12},{20,16},{24,20},{28,24},{32,28},{36,32}... | collective-permute-start | bytes 6291464 | tf_op jit(solution)/shard_map/ppermute | solution.py:40
  49.4 1.1 collective-permute-start.1
  50.5 1.7 %reshape.453 = f32[1,16,1024]{2,1,0:T(8,128)} reshape(f32[16,32,32]{2,1,0:T(8,128)} %get-tuple-element.9) | data formatting | bytes 131072 | tf_op jit(solution)/shard_map/reshape | solution.py:270
  52.3 1.0 slice.51
  53.2 0.1 concatenate.158
  53.4 42.7 %collective-permute-done.1 = f32[32,1024]{1,0:T(8,128)S(1)} collective-permute-done((f32[32,1024]{1,0:T(8,128)}, f32[32,1024]{1,0:T(8,128)S(1)}, u32[]{:S(2)}, u32[]{:S(2)}) %collective-permute-start.1) | collective-permute-done | bytes 131104 | tf_op jit(solution)/shard_map/ppermute | solution.py:40
  96.0 1.2 %convolution_multiply_fusion.1 = f32[32,32]{1,0:T(8,128)S(1)} fusion(f32[32,1024]{1,0:T(8,128)} %get-tuple-element.13, f32[32,1024]{1,0:T(8,128)S(1)} %collective-permute-done.1), kind=kOutput, calls=%fused_computation.1 | convolution fusion | flops 12583936 | bytes 266240 | tf_op jit(solution)/shard_map/dot_general | solution.py:104
  97.2 0.1 concatenate.159
  97.3 0.6 pad_maximum_fusion
  97.9 11.3 %collective-permute-done = f32[16,32,1024]{2,1,0:T(8,128)S(1)} collective-permute-done((f32[16,32,1024]{2,1,0:T(8,128)}, f32[16,32,1024]{2,1,0:T(8,128)S(1)}, u32[]{:S(2)}, u32[]{:S(2)}) %collective-permute-start) | collective-permute-done | bytes 2097184 | tf_op jit(solution)/shard_map/ppermute | solution.py:40
  109.2 3.6 %convolution_multiply_fusion = f32[16,32,32]{2,1,0:T(8,128)S(1)} fusion(f32[16,32,1024]{2,1,0:T(8,128)} %get-tuple-element.10, f32[16,32,1024]{2,1,0:T(8,128)S(1)} %collective-permute-done), kind=kOutput, calls=%fused_computation | convolution fusion | flops 201342976 | bytes 4259840 | tf_op jit(solution)/shard_map/bkc,blc->bkl/dot_general | solution.py:265
  112.9 0.8 reshape.454
  (11 shorter events, 0.1 us)
Async XLA Ops:
  0.6 4.4 %copy-start = (f32[1,16,16,256]{3,2,1,0:T(8,128)S(1)}, f32[1,16,16,256]{3,2,1,0:T(8,128)}, u32[]{:S(2)}) copy-start(f32[1,16,16,256]{3,2,1,0:T(8,128)} %param.5) | copy-start | bytes 786436
  7.1 1.3 %copy-start.1 = (f32[16,8,16,256]{3,2,1,0:T(8,128)}, f32[16,8,16,256]{3,2,1,0:T(8,128)S(1)}, u32[]{:S(2)}) copy-start(f32[16,8,16,256]{3,2,1,0:T(8,128)S(1)} %fusion.10.terms_ref) | copy-start | bytes 6291460
  44.8 64.5 %collective-permute-start = (f32[16,32,1024]{2,1,0:T(8,128)}, f32[16,32,1024]{2,1,0:T(8,128)S(1)}, u32[]{:S(2)}, u32[]{:S(2)}) collective-permute-start(f32[16,32,1024]{2,1,0:T(8,128)} %get-tuple-element.11), channel_id=1, source_target_pairs={{4,0},{8,4},{12,8},{16,12},{20,16},{24,20},{28,24},{32,28},{36,32}... | collective-permute-start | bytes 6291464 | tf_op jit(solution)/shard_map/ppermute | solution.py:40
  49.4 46.6 %collective-permute-start.1 = (f32[32,1024]{1,0:T(8,128)}, f32[32,1024]{1,0:T(8,128)S(1)}, u32[]{:S(2)}, u32[]{:S(2)}) collective-permute-start(f32[32,1024]{1,0:T(8,128)} %get-tuple-element.14), channel_id=1, source_target_pairs={{1,0},{2,1},{3,2},{0,3},{5,4},{6,5},{7,6},{4,7},{9,8},{10,9},{11,1... | collective-permute-start | bytes 393224 | tf_op jit(solution)/shard_map/ppermute | solution.py:40

commit v3 on v2

--- a/solution.py
+++ b/solution.py
@@ -110,11 +110,11 @@
     counts_ref, consts_ref, force_lo, force_hi, terms_ref, blend_ref,
     self_ref, up_ref, lo_ref, col_ref, front_ref, back_ref,
     snap, resid, direc, terms, behind,
-    *, edge_len, columns,
+    *, edge_len, columns, first,
 ):
     b = pl.program_id(0)
     last = pl.num_programs(0) - 1
-    count = jnp.minimum(counts_ref[b], MAX_SWEEPS)
+    count = jnp.minimum(counts_ref[first + b], MAX_SWEEPS)
     groups = columns // 8
     plane = edge_len * edge_len
     band = MARGIN * edge_len
@@ -199,41 +199,37 @@
         back_ref[...] = back
 
 
-def run_bricks(force, coefficient, counts):
-    bricks, columns, edge_len, plane = force.shape
-    diagonal, off_terms = prepare(coefficient)
-    inverse = 1.0 / diagonal
-    terms_in = jnp.stack((diagonal,) + off_terms + (inverse,), axis=1)
-    blend = partition(edge_len)
-    consts = jnp.asarray(np.array(sweep_constants(), np.float32).T)
-    force2 = force.reshape(bricks, columns * edge_len, plane)
-    kernel = functools.partial(brick_kernel, edge_len=edge_len, columns=columns)
+def run_chunk(force2, terms_in, blend, consts, counts, first, size):
+    bricks, rows2, _ = force2.shape
+    edge_len, plane = blend.shape
+    columns = rows2 // edge_len
+    kernel = functools.partial(brick_kernel, edge_len=edge_len, columns=columns, first=first)
     f32 = jnp.float32
     slab = MARGIN * plane
     band = plane * (edge_len // 4)
     out_shape = (
-        jax.ShapeDtypeStruct((bricks, columns, columns), f32),
-        jax.ShapeDtypeStruct((bricks, columns, slab), f32),
-        jax.ShapeDtypeStruct((bricks, columns, slab), f32),
-        jax.ShapeDtypeStruct((bricks, columns, columns), f32),
+        jax.ShapeDtypeStruct((size, columns, columns), f32),
+        jax.ShapeDtypeStruct((size, columns, slab), f32),
+        jax.ShapeDtypeStruct((size, columns, slab), f32),
+        jax.ShapeDtypeStruct((size, columns, columns), f32),
         jax.ShapeDtypeStruct((columns, band), f32),
         jax.ShapeDtypeStruct((columns, band), f32),
     )
     grid_spec = pltpu.PrefetchScalarGridSpec(
         num_scalar_prefetch=1,
-        grid=(bricks,),
+        grid=(size,),
         in_specs=[
             pl.BlockSpec(memory_space=pltpu.SMEM),
-            pl.BlockSpec((None, columns * edge_len, 128), lambda b, c: (b, 0, 0)),
-            pl.BlockSpec((None, columns * edge_len, 128), lambda b, c: (b, 0, 1)),
-            pl.BlockSpec((None, 8, edge_len, plane), lambda b, c: (b, 0, 0, 0)),
+            pl.BlockSpec((None, rows2, 128), lambda b, c: (first + b, 0, 0)),
+            pl.BlockSpec((None, rows2, 128), lambda b, c: (first + b, 0, 1)),
+            pl.BlockSpec((None, 8, edge_len, plane), lambda b, c: (first + b, 0, 0, 0)),
             pl.BlockSpec((edge_len, plane), lambda b, c: (0, 0)),
         ],
         out_specs=[
             pl.BlockSpec((None, columns, columns), lambda b, c: (b, 0, 0)),
             pl.BlockSpec((None, columns, slab), lambda b, c: (b, 0, 0)),
             pl.BlockSpec((None, columns, slab), lambda b, c: (b, 0, 0)),
-            pl.BlockSpec((bricks, columns, columns), lambda b, c: (0, 0, 0)),
+            pl.BlockSpec((size, columns, columns), lambda b, c: (0, 0, 0)),
             pl.BlockSpec((columns, band), lambda b, c: (0, 0)),
             pl.BlockSpec((columns, band), lambda b, c: (0, 0)),
         ],
@@ -245,32 +241,63 @@
             pltpu.VMEM((columns, band), f32),
         ],
     )
+    flops = size * (columns * plane * edge_len * 40 + 2 * columns * columns * plane * edge_len * 6)
     return pl.pallas_call(
         kernel,
         grid_spec=grid_spec,
         out_shape=out_shape,
         compiler_params=pltpu.CompilerParams(dimension_semantics=("arbitrary",)),
+        cost_estimate=pl.CostEstimate(
+            flops=flops, transcendentals=0, bytes_accessed=size * columns * plane * edge_len * 4
+        ),
     )(counts, consts, force2, force2, terms_in, blend)
 
 
+CHUNK = 4
+
+
 def on_device(force_columns, coefficient, sweep_counts):
-    bricks = force_columns.shape[1]
-    columns = force_columns.shape[2]
-    edge_len = force_columns.shape[3]
+    force = force_columns[0]
+    bricks, columns, edge_len, plane = force.shape
     scale_pair = (MARGIN * edge_len * edge_len) ** (-0.5)
-    self_part, upper, lower, col_part, front, back = run_bricks(
-        force_columns[0], coefficient[0], sweep_counts[0]
-    )
-    below = from_behind(upper, "wide", -1)
-    row_part = jnp.einsum("bkc,blc->bkl", lower, below, precision=HIGHEST) * scale_pair
-    arrived = from_behind(front, "narrow", -1)
-    last_col = gram(back, arrived) * scale_pair
-    col_part = jnp.concatenate([col_part[:-1], last_col[None]], axis=0)
+    diagonal, off_terms = prepare(coefficient[0])
+    inverse = 1.0 / diagonal
+    terms_in = jnp.stack((diagonal,) + off_terms + (inverse,), axis=1)
+    blend = partition(edge_len)
+    consts = jnp.asarray(np.array(sweep_constants(), np.float32).T)
+    force2 = force.reshape(bricks, columns * edge_len, plane)
+    counts = sweep_counts[0]
+    size = CHUNK if bricks % CHUNK == 0 else bricks
+    selfs, cols, fronts, backs, rows = [], [], [], [], []
+    for first in range(0, bricks, size):
+        s_c, up_c, lo_c, col_c, front_c, back_c = run_chunk(
+            force2, terms_in, blend, consts, counts, first, size
+        )
+        up_in = from_behind(up_c, "wide", -1)
+        rows.append(gram3(lo_c, up_in) * scale_pair)
+        selfs.append(s_c)
+        cols.append(col_c)
+        fronts.append(front_c)
+        backs.append(back_c)
+    fronts.append(from_behind(fronts[0], "narrow", -1))
+    joins = gram3(jnp.stack(backs), jnp.stack(fronts[1:])) * scale_pair
+    col_parts = []
+    for c in range(len(cols)):
+        col_parts.append(cols[c][:-1])
+        col_parts.append(joins[c][None])
+    row_parts = rows
+    self_part = jnp.concatenate(selfs, axis=0)
+    row_part = jnp.concatenate(row_parts, axis=0)
+    col_part = jnp.concatenate(col_parts, axis=0)
     return (
         self_part.reshape(1, bricks, -1),
         row_part.reshape(1, bricks, -1),
         col_part.reshape(1, bricks, -1),
     )
+
+
+def gram3(a, b):
+    return jnp.einsum("bkc,blc->bkl", a, b, precision=HIGHEST)
 
 
 def solution(mesh):

time: 114 us -> 97.7 us (0.86)
  the two profiles are of different devices: /device:TPU:12 before, /device:TPU:124 now
where the time goes in v3:
time: 97.7 us; the launch traced here: 97.3 us
  Pallas kernels  57.4 us (59%)
  waiting for transfers between devices  19.8 us (20%)
  local copies, waits for them, and re-layouts  8.9 us (9%)
  matrix products  6.38 us (7%)
  other arithmetic  2.71 us (3%)
  between operations  1.12 us (1%)
    pallas_call x4, Pallas kernels, run_chunk(): pl.pallas_call(kernel, grid_spec=grid_spec, out_shape=out_shape, compiler...  57.4 us
    ppermute x5, waiting for transfers between devices, from_behind(): return lax.ppermute(block, axis, route)  19.8 us
    dot_general x5, matrix products, gram3(): return jnp.einsum('bkc,blc->bkl', a, b, precision=HIGHEST)  6.38 us
    concatenate x2, local copies, waits for them, and re-layouts, prepare(): jnp.concatenate([coefficient[..., edge_len:], coefficient[..., -edge_len:...  2.26 us
    unnamed x37, local copies, waits for them, and re-layouts  2.09 us
  transfers between devices with their start and end apart: 5, of which 2 were waited for; matrix products, arithmetic and copies ran while one was open for 7% of the time, Pallas kernels for 47%

profile of v3, /device:TPU:124, one launch (start us, length us, event | category | flops | bytes accessed | tf_op | source)
XLA Modules:
  0.0 97.3 jit_solution(4524081677610358301)
XLA Ops:
  0.6 0.0 copy-start
  0.7 1.0 %slice_bitcast_fusion.11 = (f32[16,1,1,256]{3,2,0,1:T(1,128)S(1)}, f32[16,1,1,256]{3,2,1,0:T(1,128)S(1)}) fusion(f32[16,16,256]{2,1,0:T(8,128)} %bitcast.152), kind=kLoop, calls=%fused_computation.85 | loop fusion | bytes 65536 | tf_op jit(solution)/shard_map/concatenate | solution.py:50
  1.7 1.1 %slice_bitcast_fusion.9 = (f32[16,1,16,16]{3,2,0,1:T(8,128)S(1)}, f32[16,1,16,16]{3,2,0,1:T(8,128)S(1)}) fusion(f32[16,16,256]{2,1,0:T(8,128)} %bitcast.153), kind=kLoop, calls=%fused_computation.60 | loop fusion | bytes 65536 | tf_op jit(solution)/shard_map/concatenate | solution.py:52
  2.8 1.1 %slice_bitcast_fusion.7 = (f32[16,1,16,1]{3,2,0,1:T(8,128)S(1)}, f32[16,1,16,1]{3,2,0,1:T(8,128)S(1)}) fusion(f32[16,16,256]{2,1,0:T(8,128)} %bitcast.154), kind=kLoop, calls=%fused_computation.58 | loop fusion | bytes 4096 | tf_op jit(solution)/shard_map/concatenate | solution.py:57
  3.9 1.2 %slice_bitcast_fusion.3 = (f32[16,1,16,240]{3,2,0,1:T(8,128)S(1)}, f32[16,1,16,240]{3,2,0,1:T(8,128)S(1)}) fusion(f32[16,16,256]{2,1,0:T(8,128)} %bitcast.155), kind=kLoop, calls=%fused_computation.28 | loop fusion | bytes 983040 | tf_op jit(solution)/shard_map/concatenate | solution.py:52
  5.1 0.0 copy-done
  5.1 0.1 slice_bitcast_fusion.1
  5.3 0.7 fusion.34.blend_ref
  6.0 0.4 constant_dynamic-update-slice_fusion
  6.3 0.1 bitcast_dynamic-update-slice_fusion
  6.4 0.1 select_dynamic-update-slice_fusion.4
  6.5 0.1 select_dynamic-update-slice_fusion.3
  6.7 0.1 select_dynamic-update-slice_fusion.2
  6.8 0.1 select_dynamic-update-slice_fusion.1
  6.9 0.1 select_dynamic-update-slice_fusion
  7.1 0.0 copy-start.1
  7.1 1.3 %copy-done.1 = f32[16,8,16,256]{3,2,1,0:T(8,128)} copy-done((f32[16,8,16,256]{3,2,1,0:T(8,128)}, f32[16,8,16,256]{3,2,1,0:T(8,128)S(1)}, u32[]{:S(2)}) %copy-start.1) | copy-done | bytes 2097176
  8.5 12.1 %shard_map.70 = (f32[4,32,32]{2,1,0:T(8,128)}, f32[4,32,1024]{2,1,0:T(8,128)}, f32[4,32,1024]{2,1,0:T(8,128)}, f32[4,32,32]{2,1,0:T(8,128)}, f32[32,1024]{1,0:T(8,128)}, /*index=5*/f32[32,1024]{1,0:T(8,128)}) custom-call(s32[16]{0:T(128)} %bitcast.158, f32[2,8]{1,0:T(2,128)} %constant.59.clone.consts_ref, f32[16,512,256]{2,1,0:T(8,128)} %bitcast.144, ...), custom_call_target="tpu_custom_call" | custom-call | flops 222298112 | bytes 2097152 | tf_op jit(solution)/shard_map/pallas_call | solution.py:245
  20.6 0.5 collective-permute-start.3
  21.0 15.3 %shard_map.69 = (f32[4,32,32]{2,1,0:T(8,128)}, f32[4,32,1024]{2,1,0:T(8,128)}, f32[4,32,1024]{2,1,0:T(8,128)}, f32[4,32,32]{2,1,0:T(8,128)}, f32[32,1024]{1,0:T(8,128)}, /*index=5*/f32[32,1024]{1,0:T(8,128)}) custom-call(s32[16]{0:T(128)} %bitcast.159, f32[2,8]{1,0:T(2,128)} %constant.59.clone.consts_ref, f32[16,512,256]{2,1,0:T(8,128)} %bitcast.146, ...), custom_call_target="tpu_custom_call" | custom-call | flops 222298112 | bytes 2097152 | tf_op jit(solution)/shard_map/pallas_call | solution.py:245
  36.3 0.1 collective-permute-start.2
  36.4 18.5 %shard_map.67 = (f32[4,32,32]{2,1,0:T(8,128)}, f32[4,32,1024]{2,1,0:T(8,128)}, f32[4,32,1024]{2,1,0:T(8,128)}, f32[4,32,32]{2,1,0:T(8,128)}, f32[32,1024]{1,0:T(8,128)}, /*index=5*/f32[32,1024]{1,0:T(8,128)}) custom-call(s32[16]{0:T(128)} %bitcast.160, f32[2,8]{1,0:T(2,128)} %constant.59.clone.consts_ref, f32[16,512,256]{2,1,0:T(8,128)} %bitcast.148, ...), custom_call_target="tpu_custom_call" | custom-call | flops 222298112 | bytes 2097152 | tf_op jit(solution)/shard_map/pallas_call | solution.py:245
  54.9 0.0 copy-start.6
  54.9 0.0 copy-start.7
  54.9 0.0 copy-start.8
  54.9 0.0 copy-start.12
  54.9 0.1 collective-permute-start.4
  55.0 11.6 %shard_map.68 = (f32[4,32,32]{2,1,0:T(8,128)}, f32[4,32,1024]{2,1,0:T(8,128)}, f32[4,32,1024]{2,1,0:T(8,128)}, f32[4,32,32]{2,1,0:T(8,128)}, f32[32,1024]{1,0:T(8,128)}, /*index=5*/f32[32,1024]{1,0:T(8,128)}) custom-call(s32[16]{0:T(128)} %bitcast.161, f32[2,8]{1,0:T(2,128)} %constant.59.clone.consts_ref, f32[16,512,256]{2,1,0:T(8,128)} %bitcast.150, ...), custom_call_target="tpu_custom_call" | custom-call | flops 222298112 | bytes 2097152 | tf_op jit(solution)/shard_map/pallas_call | solution.py:245
  66.6 0.0 copy-start.9
  66.7 0.1 collective-permute-start.1
  66.7 0.3 collective-permute-start
  67.0 0.9 pad_maximum_fusion
  67.9 0.0 copy-start.4
  67.9 0.8 reshape.452
  68.7 0.0 collective-permute-done.4
  68.7 0.0 copy-start.14
  68.7 0.6 copy-done.14
  69.4 1.9 %convolution_multiply_fusion = f32[4,32,32]{2,1,0:T(8,128)S(1)} fusion(f32[1,32,1024]{2,1,0:T(8,128)} %bitcast.163, f32[1,32,1024]{2,1,0:T(8,128)} %bitcast.165, f32[1,32,1024]{2,1,0:T(8,128)} %bitcast.169, f32[1,32,1024]{2,1,0:T(8,128)} %bitcast.166, f32[1,32,1024]{2,1,0:T(8,128)} %bitcast.167, f32[1,32,1024]{2,1,0:T(8,128)S(1)} %bitcast.162, ...), kind=kOutput, calls=%fused_computation | convolution fusion | flops 51122176 | bytes 1064960 | tf_op jit(solution)/shard_map/bkc,blc->bkl/dot_general | solution.py:300
  71.4 0.8 reshape.454
  72.2 0.0 collective-permute-done.3
  72.2 0.6 convolution_multiply_fusion.1
  72.8 0.0 collective-permute-done.2
  72.8 0.6 convolution_multiply_fusion.2
  73.4 11.5 %collective-permute-done.1 = f32[4,32,1024]{2,1,0:T(8,128)} collective-permute-done((f32[4,32,1024]{2,1,0:T(8,128)}, f32[4,32,1024]{2,1,0:T(8,128)}, u32[]{:S(2)}, u32[]{:S(2)}) %collective-permute-start.1) | collective-permute-done | bytes 524320 | tf_op jit(solution)/shard_map/ppermute | solution.py:40
  84.9 1.6 %convolution_multiply_fusion.3 = f32[4,32,32]{2,1,0:T(8,128)S(1)} fusion(f32[4,32,1024]{2,1,0:T(8,128)S(1)} %copy-done.5, f32[4,32,1024]{2,1,0:T(8,128)} %collective-permute-done.1), kind=kOutput, calls=%fused_computation.3 | convolution fusion | flops 50335744 | bytes 1064960 | tf_op jit(solution)/shard_map/bkc,blc->bkl/dot_general | solution.py:300
  86.5 8.3 %collective-permute-done = f32[4,32,1024]{2,1,0:T(8,128)} collective-permute-done((f32[4,32,1024]{2,1,0:T(8,128)}, f32[4,32,1024]{2,1,0:T(8,128)}, u32[]{:S(2)}, u32[]{:S(2)}) %collective-permute-start) | collective-permute-done | bytes 524320 | tf_op jit(solution)/shard_map/ppermute | solution.py:40
  94.8 1.6 %convolution_multiply_fusion.4 = f32[4,32,32]{2,1,0:T(8,128)S(1)} fusion(f32[4,32,1024]{2,1,0:T(8,128)S(1)} %copy-done.2, f32[4,32,1024]{2,1,0:T(8,128)} %collective-permute-done), kind=kOutput, calls=%fused_computation.4 | convolution fusion | flops 50335744 | bytes 1064960 | tf_op jit(solution)/shard_map/bkc,blc->bkl/dot_general | solution.py:300
  96.5 0.8 reshape.453
  (38 shorter events, 0.2 us)
Async XLA Ops:
  0.6 4.4 %copy-start = (f32[1,16,16,256]{3,2,1,0:T(8,128)S(1)}, f32[1,16,16,256]{3,2,1,0:T(8,128)}, u32[]{:S(2)}) copy-start(f32[1,16,16,256]{3,2,1,0:T(8,128)} %param.5) | copy-start | bytes 786436
  7.1 1.4 %copy-start.1 = (f32[16,8,16,256]{3,2,1,0:T(8,128)}, f32[16,8,16,256]{3,2,1,0:T(8,128)S(1)}, u32[]{:S(2)}) copy-start(f32[16,8,16,256]{3,2,1,0:T(8,128)S(1)} %fusion.24.terms_ref) | copy-start | bytes 6291460
  20.6 51.6 %collective-permute-start.3 = (f32[4,32,1024]{2,1,0:T(8,128)}, f32[4,32,1024]{2,1,0:T(8,128)S(1)}, u32[]{:S(2)}, u32[]{:S(2)}) collective-permute-start(f32[4,32,1024]{2,1,0:T(8,128)} %get-tuple-element.38), channel_id=1, source_target_pairs={{4,0},{8,4},{12,8},{16,12},{20,16},{24,20},{28,24},{32,28},{36,32}... | collective-permute-start | bytes 1572872 | tf_op jit(solution)/shard_map/ppermute | solution.py:40
  36.3 36.5 %collective-permute-start.2 = (f32[4,32,1024]{2,1,0:T(8,128)}, f32[4,32,1024]{2,1,0:T(8,128)S(1)}, u32[]{:S(2)}, u32[]{:S(2)}) collective-permute-start(f32[4,32,1024]{2,1,0:T(8,128)} %get-tuple-element.36), channel_id=1, source_target_pairs={{4,0},{8,4},{12,8},{16,12},{20,16},{24,20},{28,24},{32,28},{36,32}... | collective-permute-start | bytes 1572872 | tf_op jit(solution)/shard_map/ppermute | solution.py:40
  54.9 12.1 %copy-start.6 = (f32[4,32,32]{2,1,0:T(8,128)S(1)}, f32[4,32,32]{2,1,0:T(8,128)}, u32[]{:S(2)}) copy-start(f32[4,32,32]{2,1,0:T(8,128)} %get-tuple-element.30) | copy-start | bytes 49156
  54.9 12.1 %copy-start.7 = (f32[4,32,32]{2,1,0:T(8,128)S(1)}, f32[4,32,32]{2,1,0:T(8,128)}, u32[]{:S(2)}) copy-start(f32[4,32,32]{2,1,0:T(8,128)} %get-tuple-element.29) | copy-start | bytes 49156
  54.9 12.1 %copy-start.8 = (f32[4,32,32]{2,1,0:T(8,128)S(1)}, f32[4,32,32]{2,1,0:T(8,128)}, u32[]{:S(2)}) copy-start(f32[4,32,32]{2,1,0:T(8,128)} %get-tuple-element.27) | copy-start | bytes 49156
  54.9 13.8 %copy-start.12 = (f32[4,32,32]{2,1,0:T(8,128)S(1)}, f32[4,32,32]{2,1,0:T(8,128)}, u32[]{:S(2)}) copy-start(f32[4,32,32]{2,1,0:T(8,128)} %get-tuple-element.39) | copy-start | bytes 49156
  54.9 14.4 %copy-start.13 = (f32[32,1024]{1,0:T(8,128)S(1)}, f32[32,1024]{1,0:T(8,128)}, u32[]{:S(2)}) copy-start(f32[32,1024]{1,0:T(8,128)} %get-tuple-element.46) | copy-start | bytes 393220
  54.9 13.7 %collective-permute-start.4 = (f32[32,1024]{1,0:T(8,128)}, f32[32,1024]{1,0:T(8,128)S(1)}, u32[]{:S(2)}, u32[]{:S(2)}) collective-permute-start(f32[32,1024]{1,0:T(8,128)} %get-tuple-element.47), channel_id=1, source_target_pairs={{1,0},{2,1},{3,2},{0,3},{5,4},{6,5},{7,6},{4,7},{9,8},{10,9},{11,1... | collective-permute-start | bytes 393224 | tf_op jit(solution)/shard_map/ppermute | solution.py:40
  66.6 4.7 %copy-start.10 = (f32[4,32,32]{2,1,0:T(8,128)S(1)}, f32[4,32,32]{2,1,0:T(8,128)}, u32[]{:S(2)}) copy-start(f32[4,32,32]{2,1,0:T(8,128)} %get-tuple-element.49) | copy-start | bytes 49156
  66.6 4.7 %copy-start.9 = (f32[4,32,32]{2,1,0:T(8,128)S(1)}, f32[4,32,32]{2,1,0:T(8,128)}, u32[]{:S(2)}) copy-start(f32[4,32,32]{2,1,0:T(8,128)} %get-tuple-element.50) | copy-start | bytes 49156
  66.6 5.5 %copy-start.3 = (f32[4,32,1024]{2,1,0:T(8,128)S(1)}, f32[4,32,1024]{2,1,0:T(8,128)}, u32[]{:S(2)}) copy-start(f32[4,32,1024]{2,1,0:T(8,128)} %get-tuple-element.37) | copy-start | bytes 1572868
  66.7 18.2 %collective-permute-start.1 = (f32[4,32,1024]{2,1,0:T(8,128)}, f32[4,32,1024]{2,1,0:T(8,128)}, u32[]{:S(2)}, u32[]{:S(2)}) collective-permute-start(f32[4,32,1024]{2,1,0:T(8,128)} %get-tuple-element.34), channel_id=1, source_target_pairs={{4,0},{8,4},{12,8},{16,12},{20,16},{24,20},{28,24},{32,28},{36,32}... | collective-permute-start | bytes 1572872 | tf_op jit(solution)/shard_map/ppermute | solution.py:40
  66.7 28.1 %collective-permute-start = (f32[4,32,1024]{2,1,0:T(8,128)}, f32[4,32,1024]{2,1,0:T(8,128)}, u32[]{:S(2)}, u32[]{:S(2)}) collective-permute-start(f32[4,32,1024]{2,1,0:T(8,128)} %get-tuple-element.32), channel_id=1, source_target_pairs={{4,0},{8,4},{12,8},{16,12},{20,16},{24,20},{28,24},{32,28},{36,32}... | collective-permute-start | bytes 1572872 | tf_op jit(solution)/shard_map/ppermute | solution.py:40
  67.9 4.9 %copy-start.4 = (f32[4,32,1024]{2,1,0:T(8,128)S(1)}, f32[4,32,1024]{2,1,0:T(8,128)}, u32[]{:S(2)}) copy-start(f32[4,32,1024]{2,1,0:T(8,128)} %get-tuple-element.35) | copy-start | bytes 1572868
  68.7 2.6 %copy-start.11 = (f32[4,32,32]{2,1,0:T(8,128)S(1)}, f32[4,32,32]{2,1,0:T(8,128)}, u32[]{:S(2)}) copy-start(f32[4,32,32]{2,1,0:T(8,128)} %get-tuple-element.48) | copy-start | bytes 49156
  68.7 0.7 copy-start.14
  69.4 15.5 %copy-start.5 = (f32[4,32,1024]{2,1,0:T(8,128)S(1)}, f32[4,32,1024]{2,1,0:T(8,128)}, u32[]{:S(2)}) copy-start(f32[4,32,1024]{2,1,0:T(8,128)} %get-tuple-element.33) | copy-start | bytes 1572868
  71.3 23.6 %copy-start.2 = (f32[4,32,1024]{2,1,0:T(8,128)S(1)}, f32[4,32,1024]{2,1,0:T(8,128)}, u32[]{:S(2)}) copy-start(f32[4,32,1024]{2,1,0:T(8,128)} %get-tuple-element.31) | copy-start | bytes 1572868

commit v4 on v3

--- a/solution.py
+++ b/solution.py
@@ -100,6 +100,15 @@
     return ramp(x_float, edge_len) * ramp(y_float, edge_len)
 
 
+def blend_weights(edge_len):
+    at = np.arange(edge_len, dtype=np.float32)
+    lo = (at + np.float32(0.5)) / np.float32(MARGIN)
+    hi = (np.float32(edge_len) - at - np.float32(0.5)) / np.float32(MARGIN)
+    ramp_np = np.minimum(np.float32(1.0), np.minimum(lo, hi)).astype(np.float32)
+    y_of = np.arange(edge_len * edge_len) // edge_len
+    return (ramp_np[:, None] * ramp_np[y_of][None, :]).astype(np.float32)
+
+
 def gram(a, b):
     return lax.dot_general(
         a, b, (((1,), (1,)), ((), ())), precision=HIGHEST, preferred_element_type=jnp.float32
@@ -107,7 +116,7 @@
 
 
 def brick_kernel(
-    counts_ref, consts_ref, force_lo, force_hi, terms_ref, blend_ref,
+    counts_ref, consts_ref, force_lo, force_hi, coef_ref, blend_ref,
     self_ref, up_ref, lo_ref, col_ref, front_ref, back_ref,
     snap, resid, direc, terms, behind,
     *, edge_len, columns, first,
@@ -123,9 +132,36 @@
     def rep(row):
         return jnp.concatenate([row] * groups, axis=0)
 
+    coef = coef_ref[...]
+    x_at = lax.broadcasted_iota(jnp.int32, (edge_len, plane), 0)
+    flat = lax.broadcasted_iota(jnp.int32, (edge_len, plane), 1)
+    y_at = flat // edge_len
+    z_at = flat % edge_len
+    nbrs = (
+        jnp.where(x_at == edge_len - 1, coef, pltpu.roll(coef, edge_len - 1, 0)),
+        jnp.where(x_at == 0, coef, pltpu.roll(coef, 1, 0)),
+        jnp.where(y_at == edge_len - 1, coef, pltpu.roll(coef, plane - edge_len, 1)),
+        jnp.where(y_at == 0, coef, pltpu.roll(coef, edge_len, 1)),
+        jnp.where(z_at == edge_len - 1, coef, pltpu.roll(coef, plane - 1, 1)),
+        jnp.where(z_at == 0, coef, pltpu.roll(coef, 1, 1)),
+    )
+    faces = [(coef + nb) * 0.5 for nb in nbrs]
+    diagonal = REACTION + faces[0]
+    for face in faces[1:]:
+        diagonal = diagonal + face
+    keeps = (
+        x_at < edge_len - 1, x_at > 0, y_at < edge_len - 1, y_at > 0, z_at < edge_len - 1, z_at > 0,
+    )
+    offs = [jnp.where(keep, face, 0.0) for keep, face in zip(keeps, faces)]
+    rows_all = [diagonal] + offs + [1.0 / diagonal]
     for k in range(8):
         for x in range(edge_len):
-            terms[k, x] = jnp.broadcast_to(terms_ref[k, x : x + 1, :], (8, plane))
+            terms[k, x] = jnp.broadcast_to(rows_all[k][x : x + 1, :], (8, plane))
+
+    def zroll(v, shift):
+        return jnp.concatenate(
+            [pltpu.roll(v[:, :128], shift, 1), pltpu.roll(v[:, 128:], shift, 1)], axis=1
+        )
 
     start_scale = float(np.float32(1.0 / CENTRE))
     for x in range(edge_len):
@@ -149,12 +185,12 @@
                 res = res - rep(terms[2, x]) * prev
             res = res - rep(terms[3, x]) * pltpu.roll(cur, plane - edge_len, 1)
             res = res - rep(terms[4, x]) * pltpu.roll(cur, edge_len, 1)
-            res = res - rep(terms[5, x]) * pltpu.roll(cur, plane - 1, 1)
-            res = res - rep(terms[6, x]) * pltpu.roll(cur, 1, 1)
+            res = res - rep(terms[5, x]) * zroll(cur, 127)
+            res = res - rep(terms[6, x]) * zroll(cur, 1)
             r = resid[x] - res
             resid[x] = r
             snap[x] = snap[x] + cur
-            direc[x] = keep * cur + push * (r * rep(terms[7, x]))
+            direc[x] = keep * cur + rep(push * terms[7, x]) * r
             prev, cur = cur, nxt
         return carry
 
@@ -199,7 +235,7 @@
         back_ref[...] = back
 
 
-def run_chunk(force2, terms_in, blend, consts, counts, first, size):
+def run_chunk(force2, coef, blend, consts, counts, first, size):
     bricks, rows2, _ = force2.shape
     edge_len, plane = blend.shape
     columns = rows2 // edge_len
@@ -222,7 +258,7 @@
             pl.BlockSpec(memory_space=pltpu.SMEM),
             pl.BlockSpec((None, rows2, 128), lambda b, c: (first + b, 0, 0)),
             pl.BlockSpec((None, rows2, 128), lambda b, c: (first + b, 0, 1)),
-            pl.BlockSpec((None, 8, edge_len, plane), lambda b, c: (first + b, 0, 0, 0)),
+            pl.BlockSpec((None, edge_len, plane), lambda b, c: (first + b, 0, 0)),
             pl.BlockSpec((edge_len, plane), lambda b, c: (0, 0)),
         ],
         out_specs=[
@@ -250,28 +286,26 @@
         cost_estimate=pl.CostEstimate(
             flops=flops, transcendentals=0, bytes_accessed=size * columns * plane * edge_len * 4
         ),
-    )(counts, consts, force2, force2, terms_in, blend)
-
-
-CHUNK = 4
+    )(counts, consts, force2, force2, coef, blend)
+
+
+CHUNKS = (6, 4, 4, 2)
 
 
 def on_device(force_columns, coefficient, sweep_counts):
     force = force_columns[0]
     bricks, columns, edge_len, plane = force.shape
     scale_pair = (MARGIN * edge_len * edge_len) ** (-0.5)
-    diagonal, off_terms = prepare(coefficient[0])
-    inverse = 1.0 / diagonal
-    terms_in = jnp.stack((diagonal,) + off_terms + (inverse,), axis=1)
-    blend = partition(edge_len)
+    blend = jnp.asarray(blend_weights(edge_len))
     consts = jnp.asarray(np.array(sweep_constants(), np.float32).T)
     force2 = force.reshape(bricks, columns * edge_len, plane)
     counts = sweep_counts[0]
-    size = CHUNK if bricks % CHUNK == 0 else bricks
+    sizes = CHUNKS if sum(CHUNKS) == bricks else (bricks,)
+    firsts = [sum(sizes[:i]) for i in range(len(sizes))]
     selfs, cols, fronts, backs, rows = [], [], [], [], []
-    for first in range(0, bricks, size):
+    for first, size in zip(firsts, sizes):
         s_c, up_c, lo_c, col_c, front_c, back_c = run_chunk(
-            force2, terms_in, blend, consts, counts, first, size
+            force2, coefficient[0], blend, consts, counts, first, size
         )
         up_in = from_behind(up_c, "wide", -1)
         rows.append(gram3(lo_c, up_in) * scale_pair)

time: 97.7 us -> 91 us (0.931)
  the two profiles are of different devices: /device:TPU:124 before, /device:TPU:1 now
where the time goes in v4:
time: 91 us; the launch traced here: 90.4 us
  Pallas kernels  42.4 us (47%)
  waiting for transfers between devices  22.6 us (25%)
  starting transfers between devices  11.7 us (13%)
  matrix products  6.36 us (7%)
  local copies, waits for them, and re-layouts  5.56 us (6%)
  other arithmetic  0.96 us (1%)
    pallas_call x4, Pallas kernels, run_chunk(): pl.pallas_call(kernel, grid_spec=grid_spec, out_shape=out_shape, compiler...  42.4 us
    ppermute x5, waiting for transfers between devices, from_behind(): return lax.ppermute(block, axis, route)  22.6 us
    ppermute x5, starting transfers between devices, from_behind(): return lax.ppermute(block, axis, route)  11.7 us
    dot_general x5, matrix products, gram3(): return jnp.einsum('bkc,blc->bkl', a, b, precision=HIGHEST)  6.36 us
    unnamed x17, local copies, waits for them, and re-layouts  3.25 us
  transfers between devices with their start and end apart: 5, of which 2 were waited for; matrix products, arithmetic and copies ran while one was open for 11% of the time, Pallas kernels for 40%

profile of v4, /device:TPU:1, one launch (start us, length us, event | category | flops | bytes accessed | tf_op | source)
XLA Modules:
  0.0 90.4 jit_solution(7726793949483748580)
XLA Ops:
  0.6 6.5 %shard_map.79 = (f32[2,32,32]{2,1,0:T(8,128)}, f32[2,32,1024]{2,1,0:T(8,128)}, f32[2,32,1024]{2,1,0:T(8,128)}, f32[2,32,32]{2,1,0:T(8,128)}, f32[32,1024]{1,0:T(8,128)}, /*index=5*/f32[32,1024]{1,0:T(8,128)}) custom-call(s32[16]{0:T(128)} %bitcast.31, f32[2,8]{1,0:T(2,128)} %constant.2.clone.consts_ref, f32[16,512,256]{2,1,0:T(8,128)} %bitcast.19, ...), custom_call_target="tpu_custom_call" | custom-call | flops 111149056 | bytes 1048576 | tf_op jit(solution)/shard_map/pallas_call | solution.py:281
  7.2 7.9 %collective-permute-start.3 = (f32[2,32,1024]{2,1,0:T(8,128)}, f32[2,32,1024]{2,1,0:T(8,128)}, u32[]{:S(2)}, u32[]{:S(2)}) collective-permute-start(f32[2,32,1024]{2,1,0:T(8,128)} %get-tuple-element.38), channel_id=1, source_target_pairs={{4,0},{8,4},{12,8},{16,12},{20,16},{24,20},{28,24},{32,28},{36,32}... | collective-permute-start | bytes 786440 | tf_op jit(solution)/shard_map/ppermute | solution.py:40
  15.0 10.1 %shard_map.78 = (f32[4,32,32]{2,1,0:T(8,128)}, f32[4,32,1024]{2,1,0:T(8,128)}, f32[4,32,1024]{2,1,0:T(8,128)}, f32[4,32,32]{2,1,0:T(8,128)}, f32[32,1024]{1,0:T(8,128)}, /*index=5*/f32[32,1024]{1,0:T(8,128)}) custom-call(s32[16]{0:T(128)} %bitcast.32, f32[2,8]{1,0:T(2,128)} %constant.2.clone.consts_ref, f32[16,512,256]{2,1,0:T(8,128)} %bitcast.21, ...), custom_call_target="tpu_custom_call" | custom-call | flops 222298112 | bytes 2097152 | tf_op jit(solution)/shard_map/pallas_call | solution.py:281
  25.1 0.2 collective-permute-start.2
  25.3 10.8 %shard_map.77 = (f32[4,32,32]{2,1,0:T(8,128)}, f32[4,32,1024]{2,1,0:T(8,128)}, f32[4,32,1024]{2,1,0:T(8,128)}, f32[4,32,32]{2,1,0:T(8,128)}, f32[32,1024]{1,0:T(8,128)}, /*index=5*/f32[32,1024]{1,0:T(8,128)}) custom-call(s32[16]{0:T(128)} %bitcast.33, f32[2,8]{1,0:T(2,128)} %constant.2.clone.consts_ref, f32[16,512,256]{2,1,0:T(8,128)} %bitcast.23, ...), custom_call_target="tpu_custom_call" | custom-call | flops 222298112 | bytes 2097152 | tf_op jit(solution)/shard_map/pallas_call | solution.py:281
  36.1 0.0 copy-start.3
  36.1 0.0 copy-start.4
  36.1 0.0 copy-start.2
  36.1 0.0 copy-start
  36.1 0.0 copy-start.1
  36.1 2.4 %collective-permute-start.1 = (f32[4,32,1024]{2,1,0:T(8,128)}, f32[4,32,1024]{2,1,0:T(8,128)S(1)}, u32[]{:S(2)}, u32[]{:S(2)}) collective-permute-start(f32[4,32,1024]{2,1,0:T(8,128)} %get-tuple-element.34), channel_id=1, source_target_pairs={{4,0},{8,4},{12,8},{16,12},{20,16},{24,20},{28,24},{32,28},{36,32}... | collective-permute-start | bytes 1572872 | tf_op jit(solution)/shard_map/ppermute | solution.py:40
  38.6 15.0 %shard_map.76 = (f32[6,32,32]{2,1,0:T(8,128)}, f32[6,32,1024]{2,1,0:T(8,128)}, f32[6,32,1024]{2,1,0:T(8,128)}, f32[6,32,32]{2,1,0:T(8,128)}, f32[32,1024]{1,0:T(8,128)}, /*index=5*/f32[32,1024]{1,0:T(8,128)}) custom-call(s32[16]{0:T(128)} %bitcast.34, f32[2,8]{1,0:T(2,128)} %constant.2.clone.consts_ref, f32[16,512,256]{2,1,0:T(8,128)} %bitcast.25, ...), custom_call_target="tpu_custom_call" | custom-call | flops 333447168 | bytes 3145728 | tf_op jit(solution)/shard_map/pallas_call | solution.py:281
  53.6 1.2 %collective-permute-start.4 = (f32[32,1024]{1,0:T(8,128)}, f32[32,1024]{1,0:T(8,128)}, u32[]{:S(2)}, u32[]{:S(2)}) collective-permute-start(f32[32,1024]{1,0:T(8,128)} %get-tuple-element.47), channel_id=1, source_target_pairs={{1,0},{2,1},{3,2},{0,3},{5,4},{6,5},{7,6},{4,7},{9,8},{10,9},{11,1... | collective-permute-start | bytes 393224 | tf_op jit(solution)/shard_map/ppermute | solution.py:40
  54.9 0.0 collective-permute-start
  54.9 0.0 copy-done.3
  54.9 0.0 copy-done.4
  54.9 0.9 %pad_maximum_fusion = f32[16,32,32]{2,1,0:T(8,128)S(1)} fusion(f32[2,32,32]{2,1,0:T(8,128)} %get-tuple-element.30, f32[4,32,32]{2,1,0:T(8,128)S(1)} %copy-done.3, f32[4,32,32]{2,1,0:T(8,128)S(1)} %copy-done.4, f32[6,32,32]{2,1,0:T(8,128)} %get-tuple-element.27), kind=kLoop, calls=%fused_computation.19 | loop fusion | flops 49152 | bytes 131072 | tf_op jit(solution)/shard_map/concatenate | solution.py:323
  55.8 0.8 reshape.15
  56.6 0.9 slice_dynamic-update-slice_fusion
  57.5 18.9 %collective-permute-done.4 = f32[32,1024]{1,0:T(8,128)} collective-permute-done((f32[32,1024]{1,0:T(8,128)}, f32[32,1024]{1,0:T(8,128)}, u32[]{:S(2)}, u32[]{:S(2)}) %collective-permute-start.4) | collective-permute-done | bytes 131104 | tf_op jit(solution)/shard_map/ppermute | solution.py:40
  76.3 1.9 %convolution_multiply_fusion.1 = f32[4,32,32]{2,1,0:T(8,128)S(1)} fusion(f32[1,32,1024]{2,1,0:T(8,128)} %bitcast.36, f32[1,32,1024]{2,1,0:T(8,128)} %bitcast.38, f32[1,32,1024]{2,1,0:T(8,128)} %bitcast.40, f32[1,32,1024]{2,1,0:T(8,128)} %bitcast.41, f32[1,32,1024]{2,1,0:T(8,128)} %bitcast.10, f32[1,32,1024]{2,1,0:T(8,128)} %bitcast.35, ...), kind=kOutput, calls=%fused_computation.1 | convolution fusion | flops 51122176 | bytes 1064960 | tf_op jit(solution)/shard_map/bkc,blc->bkl/dot_general | solution.py:334
  78.2 0.8 slice_dynamic-update-slice_fusion.2
  79.0 0.8 slice_dynamic-update-slice_fusion.1
  79.8 0.7 constant_dynamic-update-slice_fusion.1
  80.6 0.8 reshape.17
  81.3 0.0 collective-permute-done.3
  81.3 0.0 copy-done.2
  81.3 1.3 %convolution_multiply_fusion.4 = f32[2,32,32]{2,1,0:T(8,128)S(1)} fusion(f32[2,32,1024]{2,1,0:T(8,128)S(1)} %copy-done.2, f32[2,32,1024]{2,1,0:T(8,128)} %collective-permute-done.3), kind=kOutput, calls=%fused_computation.4 | convolution fusion | flops 25167872 | bytes 532480 | tf_op jit(solution)/shard_map/bkc,blc->bkl/dot_general | solution.py:334
  82.6 0.0 collective-permute-done.2
  82.7 0.0 copy-done
  82.7 0.6 convolution_multiply_fusion.2
  83.3 0.0 collective-permute-done.1
  83.3 0.0 copy-done.1
  83.3 0.6 convolution_multiply_fusion.3
  83.9 3.7 %collective-permute-done = f32[6,32,1024]{2,1,0:T(8,128)S(1)} collective-permute-done((f32[6,32,1024]{2,1,0:T(8,128)}, f32[6,32,1024]{2,1,0:T(8,128)S(1)}, u32[]{:S(2)}, u32[]{:S(2)}) %collective-permute-start) | collective-permute-done | bytes 786464 | tf_op jit(solution)/shard_map/ppermute | solution.py:40
  87.6 2.0 %convolution_multiply_fusion = f32[6,32,32]{2,1,0:T(8,128)S(1)} fusion(f32[6,32,1024]{2,1,0:T(8,128)} %get-tuple-element.31, f32[6,32,1024]{2,1,0:T(8,128)S(1)} %collective-permute-done), kind=kOutput, calls=%fused_computation | convolution fusion | flops 75503616 | bytes 1597440 | tf_op jit(solution)/shard_map/bkc,blc->bkl/dot_general | solution.py:334
  89.6 0.8 reshape.16
  (5 shorter events, 0.0 us)
Async XLA Ops:
  7.2 74.2 %collective-permute-start.3 = (f32[2,32,1024]{2,1,0:T(8,128)}, f32[2,32,1024]{2,1,0:T(8,128)}, u32[]{:S(2)}, u32[]{:S(2)}) collective-permute-start(f32[2,32,1024]{2,1,0:T(8,128)} %get-tuple-element.38), channel_id=1, source_target_pairs={{4,0},{8,4},{12,8},{16,12},{20,16},{24,20},{28,24},{32,28},{36,32}... | collective-permute-start | bytes 786440 | tf_op jit(solution)/shard_map/ppermute | solution.py:40
  25.1 57.5 %collective-permute-start.2 = (f32[4,32,1024]{2,1,0:T(8,128)}, f32[4,32,1024]{2,1,0:T(8,128)S(1)}, u32[]{:S(2)}, u32[]{:S(2)}) collective-permute-start(f32[4,32,1024]{2,1,0:T(8,128)} %get-tuple-element.36), channel_id=1, source_target_pairs={{4,0},{8,4},{12,8},{16,12},{20,16},{24,20},{28,24},{32,28},{36,32}... | collective-permute-start | bytes 1572872 | tf_op jit(solution)/shard_map/ppermute | solution.py:40
  36.1 18.8 %copy-start.3 = (f32[4,32,32]{2,1,0:T(8,128)S(1)}, f32[4,32,32]{2,1,0:T(8,128)}, u32[]{:S(2)}) copy-start(f32[4,32,32]{2,1,0:T(8,128)} %get-tuple-element.29) | copy-start | bytes 49156
  36.1 18.8 %copy-start.4 = (f32[4,32,32]{2,1,0:T(8,128)S(1)}, f32[4,32,32]{2,1,0:T(8,128)}, u32[]{:S(2)}) copy-start(f32[4,32,32]{2,1,0:T(8,128)} %get-tuple-element.28) | copy-start | bytes 49156
  36.1 45.2 %copy-start.2 = (f32[2,32,1024]{2,1,0:T(8,128)S(1)}, f32[2,32,1024]{2,1,0:T(8,128)}, u32[]{:S(2)}) copy-start(f32[2,32,1024]{2,1,0:T(8,128)} %get-tuple-element.37) | copy-start | bytes 786436
  36.1 46.5 %copy-start = (f32[4,32,1024]{2,1,0:T(8,128)S(1)}, f32[4,32,1024]{2,1,0:T(8,128)}, u32[]{:S(2)}) copy-start(f32[4,32,1024]{2,1,0:T(8,128)} %get-tuple-element.35) | copy-start | bytes 1572868
  36.1 47.2 %copy-start.1 = (f32[4,32,1024]{2,1,0:T(8,128)S(1)}, f32[4,32,1024]{2,1,0:T(8,128)}, u32[]{:S(2)}) copy-start(f32[4,32,1024]{2,1,0:T(8,128)} %get-tuple-element.33) | copy-start | bytes 1572868
  36.1 47.1 %collective-permute-start.1 = (f32[4,32,1024]{2,1,0:T(8,128)}, f32[4,32,1024]{2,1,0:T(8,128)S(1)}, u32[]{:S(2)}, u32[]{:S(2)}) collective-permute-start(f32[4,32,1024]{2,1,0:T(8,128)} %get-tuple-element.34), channel_id=1, source_target_pairs={{4,0},{8,4},{12,8},{16,12},{20,16},{24,20},{28,24},{32,28},{36,32}... | collective-permute-start | bytes 1572872 | tf_op jit(solution)/shard_map/ppermute | solution.py:40
  53.6 22.7 %collective-permute-start.4 = (f32[32,1024]{1,0:T(8,128)}, f32[32,1024]{1,0:T(8,128)}, u32[]{:S(2)}, u32[]{:S(2)}) collective-permute-start(f32[32,1024]{1,0:T(8,128)} %get-tuple-element.47), channel_id=1, source_target_pairs={{1,0},{2,1},{3,2},{0,3},{5,4},{6,5},{7,6},{4,7},{9,8},{10,9},{11,1... | collective-permute-start | bytes 393224 | tf_op jit(solution)/shard_map/ppermute | solution.py:40
  54.9 32.8 %collective-permute-start = (f32[6,32,1024]{2,1,0:T(8,128)}, f32[6,32,1024]{2,1,0:T(8,128)S(1)}, u32[]{:S(2)}, u32[]{:S(2)}) collective-permute-start(f32[6,32,1024]{2,1,0:T(8,128)} %get-tuple-element.32), channel_id=1, source_target_pairs={{4,0},{8,4},{12,8},{16,12},{20,16},{24,20},{28,24},{32,28},{36,32}... | collective-permute-start | bytes 2359304 | tf_op jit(solution)/shard_map/ppermute | solution.py:40

commit v5 on v4

--- a/solution.py
+++ b/solution.py
@@ -116,10 +116,11 @@
 
 
 def brick_kernel(
-    counts_ref, consts_ref, force_lo, force_hi, coef_ref, blend_ref,
-    self_ref, up_ref, lo_ref, col_ref, front_ref, back_ref,
+    counts_ref, consts_ref, force_lo, force_hi, coef_ref, blend_ref, behind_in, arrived,
+    self_in, col_in, lo_in,
+    self_ref, col_ref, lo_ref, up_ref, front_ref, back_ref,
     snap, resid, direc, terms, behind,
-    *, edge_len, columns, first,
+    *, edge_len, columns, first, closing,
 ):
     b = pl.program_id(0)
     last = pl.num_programs(0) - 1
@@ -216,15 +217,30 @@
     front = jnp.concatenate(fronts, axis=1)
     back = jnp.concatenate(backs, axis=1)
     whole = jnp.concatenate(weighted, axis=1)
-    self_ref[...] = gram(whole, whole) / float(edge_len**3)
+    @pl.when(b == 0)
+    def _():
+        self_ref[...] = self_in[...]
+        col_ref[...] = col_in[...]
+
+    self_ref[first + b] = gram(whole, whole) / float(edge_len**3)
     up_ref[...] = jnp.concatenate(weighted[:MARGIN], axis=1)
     lo_ref[...] = jnp.concatenate(weighted[edge_len - MARGIN :], axis=1)
 
-    @pl.when(b > 0)
+    @pl.when(b == 0)
     def _():
-        col_ref[b - 1] = gram(behind[...], front) * scale_pair
-
+        behind[...] = behind_in[...]
+
+    if first == 0:
+        @pl.when(b > 0)
+        def _():
+            col_ref[b - 1] = gram(behind[...], front) * scale_pair
+    else:
+        col_ref[first + b - 1] = gram(behind[...], front) * scale_pair
     behind[...] = back
+    if closing:
+        @pl.when(b == last)
+        def _():
+            col_ref[first + last] = gram(back, arrived[...]) * scale_pair
 
     @pl.when(b == 0)
     def _():
@@ -235,22 +251,26 @@
         back_ref[...] = back
 
 
-def run_chunk(force2, coef, blend, consts, counts, first, size):
+def run_chunk(force2, coef, blend, consts, counts, behind_in, arrived, bufs, first, size):
     bricks, rows2, _ = force2.shape
     edge_len, plane = blend.shape
     columns = rows2 // edge_len
-    kernel = functools.partial(brick_kernel, edge_len=edge_len, columns=columns, first=first)
+    closing = first + size == bricks
+    kernel = functools.partial(
+        brick_kernel, edge_len=edge_len, columns=columns, first=first, closing=closing
+    )
     f32 = jnp.float32
     slab = MARGIN * plane
     band = plane * (edge_len // 4)
     out_shape = (
-        jax.ShapeDtypeStruct((size, columns, columns), f32),
+        jax.ShapeDtypeStruct((bricks, columns, columns), f32),
+        jax.ShapeDtypeStruct((bricks, columns, columns), f32),
+        jax.ShapeDtypeStruct((bricks, columns, slab), f32),
         jax.ShapeDtypeStruct((size, columns, slab), f32),
-        jax.ShapeDtypeStruct((size, columns, slab), f32),
-        jax.ShapeDtypeStruct((size, columns, columns), f32),
         jax.ShapeDtypeStruct((columns, band), f32),
         jax.ShapeDtypeStruct((columns, band), f32),
     )
+    whole = lambda b, c: (0, 0, 0)
     grid_spec = pltpu.PrefetchScalarGridSpec(
         num_scalar_prefetch=1,
         grid=(size,),
@@ -260,12 +280,17 @@
             pl.BlockSpec((None, rows2, 128), lambda b, c: (first + b, 0, 1)),
             pl.BlockSpec((None, edge_len, plane), lambda b, c: (first + b, 0, 0)),
             pl.BlockSpec((edge_len, plane), lambda b, c: (0, 0)),
+            pl.BlockSpec((columns, band), lambda b, c: (0, 0)),
+            pl.BlockSpec((columns, band), lambda b, c: (0, 0)),
+            pl.BlockSpec((bricks, columns, columns), whole),
+            pl.BlockSpec((bricks, columns, columns), whole),
+            pl.BlockSpec(memory_space=pl.ANY),
         ],
         out_specs=[
-            pl.BlockSpec((None, columns, columns), lambda b, c: (b, 0, 0)),
+            pl.BlockSpec((bricks, columns, columns), whole),
+            pl.BlockSpec((bricks, columns, columns), whole),
+            pl.BlockSpec((None, columns, slab), lambda b, c: (first + b, 0, 0)),
             pl.BlockSpec((None, columns, slab), lambda b, c: (b, 0, 0)),
-            pl.BlockSpec((None, columns, slab), lambda b, c: (b, 0, 0)),
-            pl.BlockSpec((size, columns, columns), lambda b, c: (0, 0, 0)),
             pl.BlockSpec((columns, band), lambda b, c: (0, 0)),
             pl.BlockSpec((columns, band), lambda b, c: (0, 0)),
         ],
@@ -283,10 +308,11 @@
         grid_spec=grid_spec,
         out_shape=out_shape,
         compiler_params=pltpu.CompilerParams(dimension_semantics=("arbitrary",)),
+        input_output_aliases={8: 0, 9: 1, 10: 2},
         cost_estimate=pl.CostEstimate(
             flops=flops, transcendentals=0, bytes_accessed=size * columns * plane * edge_len * 4
         ),
-    )(counts, consts, force2, force2, coef, blend)
+    )(counts, consts, force2, force2, coef, blend, behind_in, arrived, *bufs)
 
 
 CHUNKS = (6, 4, 4, 2)
@@ -302,27 +328,27 @@
     counts = sweep_counts[0]
     sizes = CHUNKS if sum(CHUNKS) == bricks else (bricks,)
     firsts = [sum(sizes[:i]) for i in range(len(sizes))]
-    selfs, cols, fronts, backs, rows = [], [], [], [], []
+    band = plane * (edge_len // 4)
+    behind = jnp.zeros((columns, band), jnp.float32)
+    blank = jnp.zeros((columns, band), jnp.float32)
+    arrived = blank
+    bufs = (
+        jnp.zeros((bricks, columns, columns), jnp.float32),
+        jnp.zeros((bricks, columns, columns), jnp.float32),
+        jnp.zeros((bricks, columns, MARGIN * plane), jnp.float32),
+    )
+    ups_in = []
     for first, size in zip(firsts, sizes):
-        s_c, up_c, lo_c, col_c, front_c, back_c = run_chunk(
-            force2, coefficient[0], blend, consts, counts, first, size
+        self_b, col_b, lo_b, up_c, front_c, behind = run_chunk(
+            force2, coefficient[0], blend, consts, counts, behind,
+            arrived if first + size == bricks else blank, bufs, first, size,
         )
-        up_in = from_behind(up_c, "wide", -1)
-        rows.append(gram3(lo_c, up_in) * scale_pair)
-        selfs.append(s_c)
-        cols.append(col_c)
-        fronts.append(front_c)
-        backs.append(back_c)
-    fronts.append(from_behind(fronts[0], "narrow", -1))
-    joins = gram3(jnp.stack(backs), jnp.stack(fronts[1:])) * scale_pair
-    col_parts = []
-    for c in range(len(cols)):
-        col_parts.append(cols[c][:-1])
-        col_parts.append(joins[c][None])
-    row_parts = rows
-    self_part = jnp.concatenate(selfs, axis=0)
-    row_part = jnp.concatenate(row_parts, axis=0)
-    col_part = jnp.concatenate(col_parts, axis=0)
+        bufs = (self_b, col_b, lo_b)
+        if first == 0:
+            arrived = from_behind(front_c, "narrow", -1)
+        ups_in.append(from_behind(up_c, "wide", -1))
+    self_part, col_part, lows = bufs
+    row_part = gram3(lows, jnp.concatenate(ups_in, axis=0)) * scale_pair
     return (
         self_part.reshape(1, bricks, -1),
         row_part.reshape(1, bricks, -1),

time: 91 us -> 106 us (1.16)
  the two profiles are of different devices: /device:TPU:1 before, /device:TPU:30 now
where the time goes in v5:
time: 106 us
  Pallas kernels  75.7 us (71%)
  waiting for transfers between devices  16.9 us (16%)
  local copies, waits for them, and re-layouts  8.57 us (8%)
  matrix products  3.61 us (3%)
    pallas_call x4, Pallas kernels, run_chunk(): pl.pallas_call(kernel, grid_spec=grid_spec, out_shape=out_shape, compiler...  75.7 us
    ppermute x5, waiting for transfers between devices, from_behind(): return lax.ppermute(block, axis, route)  16.9 us
    dot_general x1, matrix products, gram3(): return jnp.einsum('bkc,blc->bkl', a, b, precision=HIGHEST)  3.61 us
  transfers between devices with their start and end apart: 5, of which 2 were waited for; matrix products, arithmetic and copies ran while one was open for 3% of the time, Pallas kernels for 48%

profile of v5, /device:TPU:30, one launch (start us, length us, event | category | flops | bytes accessed | tf_op | source)
XLA Modules:
  0.0 105.8 jit_solution(6295872298981628472)
XLA Ops:
  0.6 0.7 broadcast_3_behind_in_arrived.2.behind_in.arrived
  1.3 0.7 broadcast_2_self_in_col_in.2.clone.col_in
  2.0 0.7 broadcast_2_self_in_col_in.2.self_in
  2.7 1.6 %broadcast_in_dim.3.lo_in = f32[16,32,1024]{2,1,0:T(8,128)} broadcast(f32[]{:T(128)} %constant.4.clone.1), dimensions={} | broadcast | bytes 2097156 | tf_op jit(solution)/shard_map/broadcast_in_dim | solution.py:338
  4.3 24.6 %shard_map.76 = (f32[16,32,32]{2,1,0:T(8,128)}, f32[16,32,32]{2,1,0:T(8,128)}, f32[16,32,1024]{2,1,0:T(8,128)}, f32[6,32,1024]{2,1,0:T(8,128)}, f32[32,1024]{1,0:T(8,128)}, /*index=5*/f32[32,1024]{1,0:T(8,128)}) custom-call(s32[16]{0:T(128)} %bitcast.16, ...), custom_call_target="tpu_custom_call", output_to_operand_aliasing={{0}: (8, {}), {1}: (9, {}), {2}: (10, {})} | custom-call | flops 333447168 | bytes 3145728 | tf_op jit(solution)/shard_map/pallas_call | solution.py:306
  28.9 0.1 collective-permute-start.1
  29.0 21.3 %shard_map.77 = (f32[16,32,32]{2,1,0:T(8,128)}, f32[16,32,32]{2,1,0:T(8,128)}, f32[16,32,1024]{2,1,0:T(8,128)}, f32[4,32,1024]{2,1,0:T(8,128)}, f32[32,1024]{1,0:T(8,128)}, /*index=5*/f32[32,1024]{1,0:T(8,128)}) custom-call(s32[16]{0:T(128)} %bitcast.17, ...), custom_call_target="tpu_custom_call", output_to_operand_aliasing={{0}: (8, {}), {1}: (9, {}), {2}: (10, {})} | custom-call | flops 222298112 | bytes 2097152 | tf_op jit(solution)/shard_map/pallas_call | solution.py:306
  50.3 0.0 copy-start.1
  50.3 0.0 copy-start.2
  50.3 17.6 %shard_map.78 = (f32[16,32,32]{2,1,0:T(8,128)}, f32[16,32,32]{2,1,0:T(8,128)}, f32[16,32,1024]{2,1,0:T(8,128)}, f32[4,32,1024]{2,1,0:T(8,128)}, f32[32,1024]{1,0:T(8,128)}, /*index=5*/f32[32,1024]{1,0:T(8,128)}) custom-call(s32[16]{0:T(128)} %bitcast.18, ...), custom_call_target="tpu_custom_call", output_to_operand_aliasing={{0}: (8, {}), {1}: (9, {}), {2}: (10, {})} | custom-call | flops 222298112 | bytes 2097152 | tf_op jit(solution)/shard_map/pallas_call | solution.py:306
  67.9 0.1 collective-permute-start.3
  68.0 0.0 copy-done.1
  68.0 0.1 collective-permute-start.2
  68.0 0.0 copy-done.2
  68.1 0.1 collective-permute-start
  68.1 13.7 %collective-permute-done.arrived = f32[32,1024]{1,0:T(8,128)S(1)} collective-permute-done((f32[32,1024]{1,0:T(8,128)S(1)}, f32[32,1024]{1,0:T(8,128)S(1)}, u32[]{:S(2)}, u32[]{:S(2)}) %collective-permute-start) | collective-permute-done | bytes 131104 | tf_op jit(solution)/shard_map/ppermute | solution.py:40
  81.9 0.0 copy-start
  81.9 0.6 copy-done
  82.5 12.2 %shard_map.79 = (f32[16,32,32]{2,1,0:T(8,128)}, f32[16,32,32]{2,1,0:T(8,128)}, f32[16,32,1024]{2,1,0:T(8,128)}, f32[2,32,1024]{2,1,0:T(8,128)}, f32[32,1024]{1,0:T(8,128)}, /*index=5*/f32[32,1024]{1,0:T(8,128)}) custom-call(s32[16]{0:T(128)} %bitcast.19, ...), custom_call_target="tpu_custom_call", output_to_operand_aliasing={{0}: (8, {}), {1}: (9, {}), {2}: (10, {})} | custom-call | flops 111149056 | bytes 1048576 | tf_op jit(solution)/shard_map/pallas_call | solution.py:306
  94.7 0.1 collective-permute-start.4
  94.8 1.7 %reshape.15 = f32[1,16,1024]{2,1,0:T(8,128)} reshape(f32[16,32,32]{2,1,0:T(8,128)} %get-tuple-element.36) | data formatting | bytes 131072 | tf_op jit(solution)/shard_map/reshape | solution.py:353
  96.5 1.7 %reshape.17 = f32[1,16,1024]{2,1,0:T(8,128)} reshape(f32[16,32,32]{2,1,0:T(8,128)} %get-tuple-element.42) | data formatting | bytes 131072 | tf_op jit(solution)/shard_map/reshape | solution.py:355
  98.3 3.1 %collective-permute-done.4 = f32[2,32,1024]{2,1,0:T(8,128)S(1)} collective-permute-done((f32[2,32,1024]{2,1,0:T(8,128)}, f32[2,32,1024]{2,1,0:T(8,128)S(1)}, u32[]{:S(2)}, u32[]{:S(2)}) %collective-permute-start.4) | collective-permute-done | bytes 262176 | tf_op jit(solution)/shard_map/ppermute | solution.py:40
  101.4 0.0 collective-permute-done.3
  101.4 0.0 collective-permute-done.2
  101.4 0.0 collective-permute-done.1
  101.4 3.6 %fusion.8 = f32[16,32,32]{2,1,0:T(8,128)S(1)} fusion(f32[16,32,1024]{2,1,0:T(8,128)} %get-tuple-element.37, f32[2,32,1024]{2,1,0:T(8,128)S(1)} %collective-permute-done.4, f32[4,32,1024]{2,1,0:T(8,128)S(1)} %collective-permute-done.3, f32[4,32,1024]{2,1,0:T(8,128)S(1)} %collective-permute-done.2, f32[6,32,1024]{2,1,0:T(8,128)S(1)} %collective-permute-done.1), kind=kOutput, calls=%fused_computation.8 | convolution fusion | flops 202915840 | bytes 4259840 | tf_op jit(solution)/shard_map/bkc,blc->bkl/dot_general | solution.py:360
  105.0 0.8 reshape.16
Async XLA Ops:
  28.9 72.5 %collective-permute-start.1 = (f32[6,32,1024]{2,1,0:T(8,128)}, f32[6,32,1024]{2,1,0:T(8,128)S(1)}, u32[]{:S(2)}, u32[]{:S(2)}) collective-permute-start(f32[6,32,1024]{2,1,0:T(8,128)} %get-tuple-element.38), channel_id=1, source_target_pairs={{4,0},{8,4},{12,8},{16,12},{20,16},{24,20},{28,24},{32,28},{36,32}... | collective-permute-start | bytes 2359304 | tf_op jit(solution)/shard_map/ppermute | solution.py:40
  50.3 17.7 %copy-start.1 = (f32[4,32,1024]{2,1,0:T(8,128)S(1)}, f32[4,32,1024]{2,1,0:T(8,128)}, u32[]{:S(2)}) copy-start(f32[4,32,1024]{2,1,0:T(8,128)} %get-tuple-element.39) | copy-start | bytes 1572868
  50.3 17.8 %copy-start.2 = (f32[32,1024]{1,0:T(8,128)S(1)}, f32[32,1024]{1,0:T(8,128)}, u32[]{:S(2)}) copy-start(f32[32,1024]{1,0:T(8,128)} %get-tuple-element.32) | copy-start | bytes 393220
  67.9 33.5 %collective-permute-start.3 = (f32[4,32,1024]{2,1,0:T(8,128)}, f32[4,32,1024]{2,1,0:T(8,128)S(1)}, u32[]{:S(2)}, u32[]{:S(2)}) collective-permute-start(f32[4,32,1024]{2,1,0:T(8,128)} %get-tuple-element.40), channel_id=1, source_target_pairs={{4,0},{8,4},{12,8},{16,12},{20,16},{24,20},{28,24},{32,28},{36,32}... | collective-permute-start | bytes 1572872 | tf_op jit(solution)/shard_map/ppermute | solution.py:40
  68.0 33.4 %collective-permute-start.2 = (f32[4,32,1024]{2,1,0:T(8,128)S(1)}, f32[4,32,1024]{2,1,0:T(8,128)S(1)}, u32[]{:S(2)}, u32[]{:S(2)}) collective-permute-start(f32[4,32,1024]{2,1,0:T(8,128)S(1)} %copy-done.1), channel_id=1, source_target_pairs={{4,0},{8,4},{12,8},{16,12},{20,16},{24,20},{28,24},{32,28},{36,32}... | collective-permute-start | bytes 1572872 | tf_op jit(solution)/shard_map/ppermute | solution.py:40
  68.1 13.8 %collective-permute-start = (f32[32,1024]{1,0:T(8,128)S(1)}, f32[32,1024]{1,0:T(8,128)S(1)}, u32[]{:S(2)}, u32[]{:S(2)}) collective-permute-start(f32[32,1024]{1,0:T(8,128)S(1)} %copy-done.2), channel_id=1, source_target_pairs={{1,0},{2,1},{3,2},{0,3},{5,4},{6,5},{7,6},{4,7},{9,8},{10,9},{11,1... | collective-permute-start | bytes 393224 | tf_op jit(solution)/shard_map/ppermute | solution.py:40
  81.9 0.7 copy-start
  94.7 6.7 %collective-permute-start.4 = (f32[2,32,1024]{2,1,0:T(8,128)}, f32[2,32,1024]{2,1,0:T(8,128)S(1)}, u32[]{:S(2)}, u32[]{:S(2)}) collective-permute-start(f32[2,32,1024]{2,1,0:T(8,128)} %get-tuple-element.41), channel_id=1, source_target_pairs={{4,0},{8,4},{12,8},{16,12},{20,16},{24,20},{28,24},{32,28},{36,32}... | collective-permute-start | bytes 786440 | tf_op jit(solution)/shard_map/ppermute | solution.py:40
